TPU v7x, 32 devices: a whole 2x2x4 slice. The times are simulated.
32 devices in a mesh: groups: 2 (over y), lat: 4 (over z), depth: 2 (over x), rock: 2 (over core).
Axes of the slice: x: 2, y: 2, z: 4, core: 2. Of those that a mesh axis runs over, the one named last changes fastest.
Arguments:
- incident: float32 [2, 128, 512], P(None, ('groups', 'lat')), parts along dimension 1, may hold values from -6 to 6
- phase: float32 [16, 128, 512], P('depth', ('groups', 'lat'), 'rock'), parts along dimension 1, may hold values from -3.140625 to 3.140625
- deviation: float32 [4], P(('groups', 'rock')), parts along dimension 0, may hold values from -0.4 to 0.4
Outputs:
- slab_exits: float32 [2, 4, 2, 128, 512], P('depth', None, 'rock', ('groups', 'lat')), parts along dimension 3
There are 2 independent parts, one for each index of `groups`. A program takes and returns all parts, laid end to end along the dimension named above; each array names one. Nothing has to cross between parts.
All inputs are finite; a program needn't handle non-finite values.
Results may differ from a plain program's by a relative error of at most 0.00002.
Values sent between devices are 32-bit elements; how exact they have to be, the bound alone decides.
No kernel may reach another device: no remote copies, remote signals or barrier semaphores. Data moves between devices by JAX's collectives and lax.ppermute only.
A program may use at most 64 MiB of HBM per device.

v0:
```python
import jax
import jax.numpy as jnp
from jax import lax
from jax.sharding import PartitionSpec as P

PLANES = 8


courant = 0.9
coupling = 0.2


def extended_2(x, sides, width):
    for axis, dim in sides:
        count, length = (lax.axis_size(axis), x.shape[dim])
        up = [(i, (i + 1) % count) for i in range(count - 1)]
        down = [(j, i) for i, j in up]
        last = lax.slice_in_dim(x, length - width, length, axis=dim)
        initial = lax.slice_in_dim(x, 0, width, axis=dim)
        before = lax.ppermute(last, axis, up)
        after = lax.ppermute(initial, axis, down)
        x = jnp.concatenate([before, x, after], axis=dim)
    return x


def shifted(block, axis, distance):
    devices = range(lax.axis_size(axis))
    route = [(i - distance, i) for i in devices if i - distance in devices]
    return lax.ppermute(block, axis, route)


def slopes(fields, cosine, sine_phase, detuning):
    inner_cells = fields[:, :, 1:-1]
    behind = fields[:, :, :-2]
    ahead_cells = fields[:, :, 2:]
    trans_real = -courant * (inner_cells[0] - behind[0]) - coupling * (
        sine_phase * inner_cells[2] + cosine * inner_cells[3]
    )
    trans_imag = -courant * (inner_cells[1] - behind[1]) + coupling * (
        cosine * inner_cells[2] - sine_phase * inner_cells[3]
    )
    bragg_real = (
        courant * (ahead_cells[2] - inner_cells[2])
        - coupling * (cosine * inner_cells[1] - sine_phase * inner_cells[0])
        - detuning * inner_cells[3]
    )
    bragg_imag = (
        courant * (ahead_cells[3] - inner_cells[3])
        + coupling * (cosine * inner_cells[0] + sine_phase * inner_cells[1])
        + detuning * inner_cells[2]
    )
    return jnp.stack([trans_real, trans_imag, bragg_real, bragg_imag])


def clip_outside(fields, offset, extent):
    position = offset + jnp.arange(fields.shape[2], dtype=jnp.int32)
    inside = (position >= 0) & (position < extent)
    return jnp.where(inside[None, None, :, None], fields, 0.0)


def advance(extended, cosine, sine_phase, detuning, offset, extent):
    slope_one = slopes(extended, cosine[1:-1], sine_phase[1:-1], detuning)
    trial_step = clip_outside(extended[:, :, 1:-1] + slope_one, offset + 1, extent)
    slope_two = slopes(trial_step, cosine[2:-2], sine_phase[2:-2], detuning)
    result = extended[:, :, 2:-2] + 0.5 * (slope_one[:, :, 1:-1] + slope_two)
    return clip_outside(result, offset + 2, extent)


def march_slab(fields, cosine_all, sine_all, detuning, offset, extent):
    extended = extended_2(fields, (("lat", 2),), 2 * PLANES)
    for plane_index in range(PLANES):
        length = extended.shape[2]
        trim_cells = 2 * plane_index
        extended = advance(
            extended,
            cosine_all[plane_index, trim_cells : trim_cells + length],
            sine_all[plane_index, trim_cells : trim_cells + length],
            detuning,
            offset - 2 * PLANES + trim_cells,
            extent,
        )
    return extended


def on_device(incident, phase, deviation):
    cell_rows = incident.shape[1]
    columns = incident.shape[2]
    angles = deviation.shape[0]
    sections = lax.axis_size("depth")
    section_index = lax.axis_index("depth")
    extent = cell_rows * lax.axis_size("lat")
    offset = lax.axis_index("lat") * cell_rows
    margin = 2 * PLANES
    blocks = 1
    full_phase = lax.all_gather(phase, "rock", axis=2, tiled=True)
    wide_phase = extended_2(full_phase, (("lat", 1),), margin)
    cosine_all = jnp.cos(wide_phase)
    sine_all = jnp.sin(wide_phase)
    detuning = deviation[:, None, None]
    block_width = columns // blocks
    incoming = jnp.zeros((4, angles, cell_rows, block_width), jnp.float32)
    slab_exits = jnp.zeros((4, angles, cell_rows, columns), jnp.float32)
    ticks = sections + blocks - 1
    for tick_index in range(ticks):
        block_lag = tick_index - section_index
        active = (block_lag >= 0) & (block_lag < blocks)
        beam_block = incident
        beam_block = beam_block[:, None]
        entrance = jnp.concatenate([beam_block, jnp.zeros_like(beam_block)], axis=0)
        fields = jnp.where(section_index == 0, entrance, incoming)
        fields = march_slab(fields, cosine_all, sine_all, detuning, offset, extent)
        slab_exits = jnp.where(active, fields, slab_exits)
        if tick_index + 1 < ticks:
            incoming = shifted(fields, "depth", 1)
    return slab_exits[None]


def solution(mesh):
    placed = (
        P(None, ("groups", "lat"), None),
        P("depth", ("groups", "lat"), "rock"),
        P(("groups", "rock")),
    )
    return jax.shard_map(
        on_device,
        mesh=mesh,
        in_specs=placed,
        out_specs=P("depth", None, "rock", ("groups", "lat"), None),
        check_vma=False,
    )
```

profile of v0, /device:TPU:18, one launch (start us, length us, event | category | flops | bytes accessed | tf_op | source)
XLA Modules:
  0.0 50.0 jit_solution(11542076290864815675)
XLA Ops:
  0.0 0.9 %pad_select_fusion = f32[4,1,16,512]{3,2,1,0:T(8,128)S(1)} fusion(f32[2,1,16,512]{3,2,1,0:T(8,128)} %bitcast.2936, pred[]{:T(512)S(6)} %eq.4), kind=kLoop, calls=%fused_computation.107 | loop fusion | flops 32768 | bytes 196609 | tf_op jit(solution)/shard_map/jit(_where)/select_n | solution.py:110
  0.9 2.4 %collective-permute-start.1 = (f32[4,1,16,512]{3,2,1,0:T(8,128)S(1)}, f32[4,1,16,512]{3,2,1,0:T(8,128)S(1)}, u32[]{:S(2)}, u32[]{:S(2)}) collective-permute-start(f32[4,1,16,512]{3,2,1,0:T(8,128)S(1)} %pad_select_fusion), channel_id=1, source_target_pairs={{4,0},{8,4},{12,8},{5,1},{9,5},{13,9},{6,2},{10,6},{14,10},{7,3},{... | collective-permute-start | bytes 393224 | tf_op jit(solution)/shard_map/ppermute | solution.py:21
  3.3 3.5 %collective-permute-start = (f32[4,1,16,512]{3,2,1,0:T(8,128)S(1)}, f32[4,1,16,512]{3,2,1,0:T(8,128)S(1)}, u32[]{:S(2)}, u32[]{:S(2)}) collective-permute-start(f32[4,1,16,512]{3,2,1,0:T(8,128)S(1)} %pad_select_fusion), channel_id=1, source_target_pairs={{0,4},{4,8},{8,12},{1,5},{5,9},{9,13},{2,6},{6,10},{10,14},{3,7},{... | collective-permute-start | bytes 393224 | tf_op jit(solution)/shard_map/ppermute | solution.py:20
  6.8 2.0 %all_gather.3 = f32[8,16,512]{2,1,0:T(8,128)S(1)} all-gather(f32[8,16,256]{2,1,0:T(8,128)S(1)} %copy-done.1), channel_id=1, replica_groups=mesh['groups'=2,'lat'=4,'depth'=2,'rock'=2] {'rock'}, dimensions={2}, use_global_device_ids=true | all-gather | bytes 393216 | tf_op jit(solution)/shard_map/all_gather | solution.py:95
  8.8 2.3 %collective-permute-start.3 = (f32[8,16,512]{2,1,0:T(8,128)S(1)}, f32[8,16,512]{2,1,0:T(8,128)S(1)}, u32[]{:S(2)}, u32[]{:S(2)}) collective-permute-start(f32[8,16,512]{2,1,0:T(8,128)S(1)} %all_gather.3), channel_id=1, source_target_pairs={{4,0},{8,4},{12,8},{5,1},{9,5},{13,9},{6,2},{10,6},{14,10},{7,3},{... | collective-permute-start | bytes 786440 | tf_op jit(solution)/shard_map/ppermute | solution.py:21
  11.1 3.5 %collective-permute-start.2 = (f32[8,16,512]{2,1,0:T(8,128)S(1)}, f32[8,16,512]{2,1,0:T(8,128)S(1)}, u32[]{:S(2)}, u32[]{:S(2)}) collective-permute-start(f32[8,16,512]{2,1,0:T(8,128)S(1)} %all_gather.3), channel_id=1, source_target_pairs={{0,4},{4,8},{8,12},{1,5},{5,9},{9,13},{2,6},{6,10},{10,14},{3,7},{... | collective-permute-start | bytes 786440 | tf_op jit(solution)/shard_map/ppermute | solution.py:20
  15.6 5.5 %collective-permute-done.2 = f32[8,16,512]{2,1,0:T(8,128)S(1)} collective-permute-done((f32[8,16,512]{2,1,0:T(8,128)S(1)}, f32[8,16,512]{2,1,0:T(8,128)S(1)}, u32[]{:S(2)}, u32[]{:S(2)}) %collective-permute-start.2) | collective-permute-done | bytes 262176 | tf_op jit(solution)/shard_map/ppermute | solution.py:20
  21.2 2.8 %fusion.646 = (f32[8,48,512]{2,1,0:T(8,128)S(1)}, f32[8,48,512]{2,1,0:T(8,128)S(1)}) fusion(f32[8,48,512]{2,1,0:T(8,128)S(1)} %constant_dynamic-update-slice_fusion), kind=kLoop, calls=%fused_computation.975 | loop fusion | bytes 2359296 | tf_op jit(solution)/shard_map/sin | solution.py:98
  24.2 0.1 fusion.6
  24.5 0.2 fusion.9
  25.3 0.1 fusion.25
  25.9 0.1 fusion.22
  26.5 0.1 fusion.41
  28.5 1.3 %collective-permute-start.4 = (f32[4,1,16,512]{3,2,0,1:T(8,128)S(1)}, f32[4,1,16,512]{3,2,0,1:T(8,128)S(1)}, u32[]{:S(2)}, u32[]{:S(2)}) collective-permute-start(f32[4,1,16,512]{3,2,0,1:T(8,128)S(1)} %fusion.68), channel_id=1, source_target_pairs={{0,2},{1,3},{4,6},{5,7},{8,10},{9,11},{12,14},{13,15},{16,18},{17,... | collective-permute-start | bytes 393224 | tf_op jit(solution)/shard_map/ppermute | solution.py:29
  29.8 5.6 %collective-permute-done.4 = f32[4,1,16,512]{3,2,0,1:T(8,128)S(1)} collective-permute-done((f32[4,1,16,512]{3,2,0,1:T(8,128)S(1)}, f32[4,1,16,512]{3,2,0,1:T(8,128)S(1)}, u32[]{:S(2)}, u32[]{:S(2)}) %collective-permute-start.4) | collective-permute-done | bytes 131104 | tf_op jit(solution)/shard_map/ppermute | solution.py:29
  35.4 2.4 %collective-permute-start.6 = (f32[4,1,16,512]{3,2,0,1:T(8,128)S(1)}, f32[4,1,16,512]{3,2,0,1:T(8,128)S(1)}, u32[]{:S(2)}, u32[]{:S(2)}) collective-permute-start(f32[4,1,16,512]{3,2,0,1:T(8,128)S(1)} %fusion.58), channel_id=1, source_target_pairs={{4,0},{8,4},{12,8},{5,1},{9,5},{13,9},{6,2},{10,6},{14,10},{7,3},{... | collective-permute-start | bytes 393224 | tf_op jit(solution)/shard_map/ppermute | solution.py:21
  37.7 3.5 %collective-permute-start.5 = (f32[4,1,16,512]{3,2,0,1:T(8,128)S(1)}, f32[4,1,16,512]{3,2,0,1:T(8,128)S(1)}, u32[]{:S(2)}, u32[]{:S(2)}) collective-permute-start(f32[4,1,16,512]{3,2,0,1:T(8,128)S(1)} %fusion.58), channel_id=1, source_target_pairs={{0,4},{4,8},{8,12},{1,5},{5,9},{9,13},{2,6},{6,10},{10,14},{3,7},{... | collective-permute-start | bytes 393224 | tf_op jit(solution)/shard_map/ppermute | solution.py:20
  41.2 1.0 %collective-permute-done.6 = f32[4,1,16,512]{3,2,0,1:T(8,128)S(1)} collective-permute-done((f32[4,1,16,512]{3,2,0,1:T(8,128)S(1)}, f32[4,1,16,512]{3,2,0,1:T(8,128)S(1)}, u32[]{:S(2)}, u32[]{:S(2)}) %collective-permute-start.6) | collective-permute-done | bytes 131104 | tf_op jit(solution)/shard_map/ppermute | solution.py:21
  42.2 2.4 %collective-permute-done.5 = f32[4,1,16,512]{3,2,0,1:T(8,128)S(1)} collective-permute-done((f32[4,1,16,512]{3,2,0,1:T(8,128)S(1)}, f32[4,1,16,512]{3,2,0,1:T(8,128)S(1)}, u32[]{:S(2)}, u32[]{:S(2)}) %collective-permute-start.5) | collective-permute-done | bytes 131104 | tf_op jit(solution)/shard_map/ppermute | solution.py:20
  45.4 0.2 fusion.4
  46.1 0.1 fusion.17
  46.8 0.1 fusion.14
  47.4 0.1 fusion.33
  49.3 0.7 %fusion.64 = f32[1,4,1,16,512]{4,3,2,1,0:T(8,128)} fusion(f32[4,1,18,512]{3,2,1,0:T(8,128)S(1)} %get-tuple-element.160, f32[4,1,20,512]{3,2,1,0:T(8,128)S(1)} %fusion.46, f32[1,1,16,512]{3,2,1,0:T(8,128)S(1)} %get-tuple-element.104, f32[1,1,16,512]{3,2,1,0:T(8,128)S(1)} %get-tuple-element.102, f32[1,1,16,512]{3,2,1,0:T(8,128)S(1)} %get-tuple-element.103, ...), kind=kLoop, calls=%fused_computation.115 | loop fusion | flops 294912 | bytes 655378 | tf_op jit(solution)/shard_map/broadcast_in_dim | solution.py:115
  (117 shorter events, 7.6 us)
Async XLA Ops:
  0.0 6.8 %copy-start.1 = (f32[8,16,256]{2,1,0:T(8,128)S(1)}, f32[8,16,256]{2,1,0:T(8,128)}, u32[]{:S(2)}) copy-start(f32[8,16,256]{2,1,0:T(8,128)} %param.4) | copy-start | bytes 393220
  0.9 14.6 %collective-permute-start.1 = (f32[4,1,16,512]{3,2,1,0:T(8,128)S(1)}, f32[4,1,16,512]{3,2,1,0:T(8,128)S(1)}, u32[]{:S(2)}, u32[]{:S(2)}) collective-permute-start(f32[4,1,16,512]{3,2,1,0:T(8,128)S(1)} %pad_select_fusion), channel_id=1, source_target_pairs={{4,0},{8,4},{12,8},{5,1},{9,5},{13,9},{6,2},{10,6},{14,10},{7,3},{... | collective-permute-start | bytes 393224 | tf_op jit(solution)/shard_map/ppermute | solution.py:21
  3.3 12.3 %collective-permute-start = (f32[4,1,16,512]{3,2,1,0:T(8,128)S(1)}, f32[4,1,16,512]{3,2,1,0:T(8,128)S(1)}, u32[]{:S(2)}, u32[]{:S(2)}) collective-permute-start(f32[4,1,16,512]{3,2,1,0:T(8,128)S(1)} %pad_select_fusion), channel_id=1, source_target_pairs={{0,4},{4,8},{8,12},{1,5},{5,9},{9,13},{2,6},{6,10},{10,14},{3,7},{... | collective-permute-start | bytes 393224 | tf_op jit(solution)/shard_map/ppermute | solution.py:20
  8.8 12.4 %collective-permute-start.3 = (f32[8,16,512]{2,1,0:T(8,128)S(1)}, f32[8,16,512]{2,1,0:T(8,128)S(1)}, u32[]{:S(2)}, u32[]{:S(2)}) collective-permute-start(f32[8,16,512]{2,1,0:T(8,128)S(1)} %all_gather.3), channel_id=1, source_target_pairs={{4,0},{8,4},{12,8},{5,1},{9,5},{13,9},{6,2},{10,6},{14,10},{7,3},{... | collective-permute-start | bytes 786440 | tf_op jit(solution)/shard_map/ppermute | solution.py:21
  11.1 10.0 %collective-permute-start.2 = (f32[8,16,512]{2,1,0:T(8,128)S(1)}, f32[8,16,512]{2,1,0:T(8,128)S(1)}, u32[]{:S(2)}, u32[]{:S(2)}) collective-permute-start(f32[8,16,512]{2,1,0:T(8,128)S(1)} %all_gather.3), channel_id=1, source_target_pairs={{0,4},{4,8},{8,12},{1,5},{5,9},{9,13},{2,6},{6,10},{10,14},{3,7},{... | collective-permute-start | bytes 786440 | tf_op jit(solution)/shard_map/ppermute | solution.py:20
  28.4 7.0 %copy-start = (f32[2,16,512]{2,1,0:T(8,128)S(1)}, f32[2,16,512]{2,1,0:T(8,128)}, u32[]{:S(2)}) copy-start(f32[2,16,512]{2,1,0:T(8,128)} %param.3) | copy-start | bytes 196612
  28.5 6.9 %collective-permute-start.4 = (f32[4,1,16,512]{3,2,0,1:T(8,128)S(1)}, f32[4,1,16,512]{3,2,0,1:T(8,128)S(1)}, u32[]{:S(2)}, u32[]{:S(2)}) collective-permute-start(f32[4,1,16,512]{3,2,0,1:T(8,128)S(1)} %fusion.68), channel_id=1, source_target_pairs={{0,2},{1,3},{4,6},{5,7},{8,10},{9,11},{12,14},{13,15},{16,18},{17,... | collective-permute-start | bytes 393224 | tf_op jit(solution)/shard_map/ppermute | solution.py:29
  35.4 6.9 %collective-permute-start.6 = (f32[4,1,16,512]{3,2,0,1:T(8,128)S(1)}, f32[4,1,16,512]{3,2,0,1:T(8,128)S(1)}, u32[]{:S(2)}, u32[]{:S(2)}) collective-permute-start(f32[4,1,16,512]{3,2,0,1:T(8,128)S(1)} %fusion.58), channel_id=1, source_target_pairs={{4,0},{8,4},{12,8},{5,1},{9,5},{13,9},{6,2},{10,6},{14,10},{7,3},{... | collective-permute-start | bytes 393224 | tf_op jit(solution)/shard_map/ppermute | solution.py:21
  37.7 6.9 %collective-permute-start.5 = (f32[4,1,16,512]{3,2,0,1:T(8,128)S(1)}, f32[4,1,16,512]{3,2,0,1:T(8,128)S(1)}, u32[]{:S(2)}, u32[]{:S(2)}) collective-permute-start(f32[4,1,16,512]{3,2,0,1:T(8,128)S(1)} %fusion.58), channel_id=1, source_target_pairs={{0,4},{4,8},{8,12},{1,5},{5,9},{9,13},{2,6},{6,10},{10,14},{3,7},{... | collective-permute-start | bytes 393224 | tf_op jit(solution)/shard_map/ppermute | solution.py:20
where the time goes:
time: 50.3 us; the launch traced here: 50 us
  starting transfers between devices  18.8 us (37%)
  waiting for transfers between devices  14.4 us (29%)
  other arithmetic  10.4 us (21%)
  local copies, waits for them, and re-layouts  2.84 us (6%)
  blocking collectives  1.99 us (4%)
  between operations  1.56 us (3%)
    ppermute x3, starting transfers between devices, extended_2(): before = lax.ppermute(last, axis, up)  10.5 us
    ppermute x3, waiting for transfers between devices, extended_2(): before = lax.ppermute(last, axis, up)  7.86 us
    ppermute x3, starting transfers between devices, extended_2(): after = lax.ppermute(initial, axis, down)  7.06 us
    ppermute x1, waiting for transfers between devices, shifted(): return lax.ppermute(block, axis, route)  5.56 us
    another operation x65, other arithmetic, slopes(): return jnp.stack([trans_real, trans_imag, bragg_real, bragg_imag])  5.03 us
    select_n x32, other arithmetic, clip_outside(): return jnp.where(inside[None, None, :, None], fields, 0.0)  3.4 us
    sin x1, local copies, waits for them, and re-layouts, on_device(): sine_all = jnp.sin(wide_phase)  2.78 us
    all_gather x1, blocking collectives, on_device(): full_phase = lax.all_gather(phase, 'rock', axis=2, tiled=True)  1.99 us
  transfers between devices with their start and end apart: 7, of which 4 were waited for; matrix products, arithmetic and copies ran while one was open for 0% of the time, Pallas kernels for 0%

commit v1 on v0

v1 whole, which is shorter than its diff:
```python
import functools
import math

import jax
import jax.numpy as jnp
import numpy as np
from jax import lax
from jax.experimental import pallas as pl
from jax.experimental.pallas import tpu as pltpu
from jax.sharding import PartitionSpec as P

courant = np.float32(0.9)
coupling = np.float32(0.2)


nu = float(courant)
stay = float(np.float32(1.0) - courant) / nu
amplitude = float(coupling) / nu
carry = 1.0 / nu**2


def half_angle_series():
    z = np.linspace(0.0, math.pi**2 * 1.0001, 20001)
    y = np.sqrt(z) / 2
    sine = np.where(y > 0, np.sin(y) / np.maximum(2 * y, 1e-30), 0.5)
    cheb, power = np.polynomial.Chebyshev, np.polynomial.Polynomial
    fits = [cheb.fit(z, v, d).convert(kind=power).coef for v, d in ((sine, 5), (np.cos(y), 6))]
    return [[float(c) for c in fit] for fit in fits]


sine_series, cosine_series = half_angle_series()


def horner(series, z):
    total = series[-1] * z + series[-2]
    for c in series[-3::-1]:
        total = total * z + c
    return total


def scaled_sincos(phi, scale):
    z = phi * phi
    s = horner(sine_series, z) * phi
    t = s * (2.0 * scale)
    return t * horner(cosine_series, z), scale - t * s


def pick(index, values):
    out = values[-1]
    for i in range(len(values) - 2, -1, -1):
        out = jnp.where(index == i, values[i], out)
    return out


def columns_at(ref, index, count, block):
    if block % 128 == 0:
        return ref[:, :, pl.ds(pl.multiple_of(index * block, block), block)]
    return pick(index, [ref[:, :, i * block : (i + 1) * block] for i in range(count)])


def pack_kernel(meta, phase, incident, *outs, sections):
    planes, rows, block = outs[0].shape
    width = 2 * planes
    own, entrance, sends = outs[0], outs[1], outs[2:]
    depth, odd = meta[0], meta[1]
    entrance[...] = columns_at(incident, meta[4] * sections + depth, incident.shape[2] // block, block)
    for shift in range(sections):
        target = lax.rem(depth + shift, sections)
        if shift == 0:
            full, even_pairs, odd_pairs = own, sends[0], sends[1]
        else:
            full, even_pairs, odd_pairs = sends[3 * shift - 1 : 3 * shift + 2]
        full[...] = columns_at(phase, target, sections, block)

        def fill(up_ref, down_ref):
            base = rows - width
            for p in range(planes // 2):
                q = planes - 1 - p
                n = 2 * p + 1
                up_ref[p] = full[p, base:rows, :]
                up_ref[p, 0:n, :] = full[q, rows - n : rows, :]
                down_ref[p] = full[p, 0:width, :]
                down_ref[p, width - n : width, :] = full[q, 0:n, :]
            if shift == 0:
                for c in range(2):
                    up_ref[planes // 2 + c] = entrance[c, base:rows, :]
                    down_ref[planes // 2 + c] = entrance[c, 0:width, :]

        @pl.when(odd == 0)
        def _():
            fill(even_pairs, odd_pairs)

        @pl.when(odd == 1)
        def _():
            fill(odd_pairs, even_pairs)


def slab_kernel(meta, detuning, *refs, sections, slab, planes, rows):
    width = 2 * planes
    odd, lower, upper = meta[1], meta[2] > 0, meta[3] > 0
    source = lax.rem(meta[0] - slab + sections, sections)
    phases, refs = refs[: 3 * sections], refs[3 * sections :]
    starts, refs = refs[:3], refs[3:]
    out, v0, v1, w, cs, ss = refs
    angles = out.shape[0]

    def side(refs_even, refs_odd, *at):
        even, odds = pick(source, [r[at] for r in refs_even]), pick(source, [r[at] for r in refs_odd])
        return jnp.where(odd == 0, odds, even), jnp.where(odd == 0, even, odds)

    full, even_pairs, odd_pairs = phases[0::3], phases[1::3], phases[2::3]
    low_scale = jnp.where(lower, amplitude, 0.0)
    high_scale = jnp.where(upper, amplitude, 0.0)
    for p in range(planes // 2):
        q = planes - 1 - p
        below, above = side(even_pairs, odd_pairs, p)
        for at, n, block, scale in (
            (0, width - 1 - 2 * p, below, low_scale),
            (width + rows, 2 * p + 1 - width, above, high_scale),
        ):
            for table, value in zip((ss, cs), scaled_sincos(block, scale)):
                table[p, at : at + width, :] = value
                table[q, at + n : at + n + width, :] = value
    for p in range(planes):
        block = pick(source, [r[p] for r in full])
        ss[p, width : width + rows, :], cs[p, width : width + rows, :] = scaled_sincos(block, amplitude)

    blank = jnp.zeros((width, out.shape[3]), jnp.float32)
    for a in range(angles):
        for c in range(4):
            if slab == 0:
                own, even_halo, odd_halo = starts
                if c < 2:
                    even, odds = even_halo[planes // 2 + c], odd_halo[planes // 2 + c]
                    middle = own[c]
                else:
                    even = odds = blank
                    middle = jnp.zeros((rows, out.shape[3]), jnp.float32)
                below, above = jnp.where(odd == 0, odds, even), jnp.where(odd == 0, even, odds)
            else:
                own, even_halo, odd_halo = starts
                middle = own[a, c]
                below = jnp.where(odd == 0, odd_halo[a, c, rows - width :, :], even_halo[a, c, rows - width :, :])
                above = jnp.where(odd == 0, even_halo[a, c, :width, :], odd_halo[a, c, :width, :])
            v0[a, c, 0:width, :] = jnp.where(lower, below, 0.0)
            v0[a, c, width : width + rows, :] = middle
            v0[a, c, width + rows : 2 * width + rows, :] = jnp.where(upper, above, 0.0)

    def euler(ref, a, at, sine, cosine, turn):
        here = slice(at, at + 8)
        tr, ti, br, bi = (ref[a, c, here, :] for c in range(4))
        tr_back, ti_back = (ref[a, c, at - 1 : at + 7, :] for c in (0, 1))
        br_next, bi_next = (ref[a, c, at + 1 : at + 9, :] for c in (2, 3))
        return (
            (stay * tr + tr_back) - (sine * br + cosine * bi),
            (stay * ti + ti_back) + (cosine * br - sine * bi),
            (stay * br + br_next) - (cosine * ti - sine * tr) - turn * bi,
            (stay * bi + bi_next) + (cosine * tr + sine * ti) + turn * br,
        )

    turns = [detuning[a] * (1.0 / nu) for a in range(angles)]
    now, later = v0, v1
    for p in range(planes):
        reach = 2 * (planes - p) - 1
        for at in range(width - reach, width + rows + reach, 8):
            sine, cosine = ss[p, at : at + 8, :], cs[p, at : at + 8, :]
            for a in range(angles):
                for c, value in enumerate(euler(now, a, at, sine, cosine, turns[a])):
                    w[a, c, at : at + 8, :] = value
        reach -= 1
        for at in range(width - reach, width + rows + reach, 8):
            sine, cosine = ss[p, at : at + 8, :], cs[p, at : at + 8, :]
            for a in range(angles):
                for c, value in enumerate(euler(w, a, at, sine, cosine, turns[a])):
                    later[a, c, at : at + 8, :] = carry * now[a, c, at : at + 8, :] + value
        now, later = later, now
    shrink = (nu**2 / 2.0) ** planes
    for a in range(angles):
        for c in range(4):
            out[a, c] = shrink * now[a, c, width : width + rows, :]


VMEM = pl.BlockSpec(memory_space=pltpu.VMEM)
SMEM = pl.BlockSpec(memory_space=pltpu.SMEM)


def neighbours(lat, sections, cores, parity, shift):
    pairs = []
    for row in range(lat):
        other = row + 1 if row % 2 == parity else row - 1
        for depth in range(sections):
            for core in range(cores):
                here = (row * sections + depth) * cores + core
                if 0 <= other < lat:
                    there = (other * sections + (depth + shift) % sections) * cores + core
                else:
                    there = (row * sections + depth) * cores + (core + 1) % cores
                pairs.append((here, there))
    return pairs


def on_device(incident, phase, deviation):
    planes, rows, columns = phase.shape
    lat, sections, cores = (lax.axis_size(a) for a in ("lat", "depth", "rock"))
    row, depth, core = (lax.axis_index(a) for a in ("lat", "depth", "rock"))
    angles = cores * deviation.shape[0]
    block = columns // sections
    width = 2 * planes
    assert rows >= width and planes % 2 == 0
    everyone = ("lat", "depth", "rock")

    def from_neighbour(value, parity, shift):
        return lax.ppermute(value, everyone, neighbours(lat, sections, cores, parity, shift))

    def route(value, shift, turn):
        pairs = []
        for d in range(sections):
            for c in range(cores):
                pairs.append((d * cores + c, (d + shift) % sections * cores + (c + turn) % cores))
        return lax.ppermute(value, ("depth", "rock"), pairs)

    meta = jnp.stack([depth, row % 2, row > 0, row + 1 < lat, core]).astype(jnp.int32)
    shape = lambda *dims: jax.ShapeDtypeStruct(dims, jnp.float32)
    outs = [shape(planes, rows, block), shape(2, rows, block)]
    outs += [shape(planes // 2 + 2, width, block)] * 2
    for _ in range(1, sections):
        outs += [shape(planes, rows, block)] + [shape(planes // 2, width, block)] * 2
    packed = pl.pallas_call(
        functools.partial(pack_kernel, sections=sections),
        out_shape=outs,
        in_specs=[SMEM, VMEM, VMEM],
        out_specs=[VMEM] * len(outs),
        name="pack",
    )(meta, phase, incident)
    own, entrance, sends = packed[0], packed[1], packed[2:]
    detuning = [deviation]
    for turn in range(1, cores):
        detuning.append(route(deviation, 0, turn))
    detuning = jnp.concatenate(detuning)
    received = [own, from_neighbour(sends[0], 0, 0), from_neighbour(sends[1], 1, 0)]
    for shift in range(1, sections):
        full, even, odd = sends[3 * shift - 1 : 3 * shift + 2]
        received += [route(full, shift, 0), from_neighbour(even, 0, shift), from_neighbour(odd, 1, shift)]

    starts = [entrance, received[1], received[2]]
    exits = []
    window = rows + 2 * width + 16
    for slab in range(sections):
        fields = pl.pallas_call(
            functools.partial(slab_kernel, sections=sections, slab=slab, planes=planes, rows=rows),
            out_shape=shape(angles, 4, rows, block),
            in_specs=[SMEM, SMEM] + [VMEM] * (len(received) + 3),
            out_specs=VMEM,
            scratch_shapes=[pltpu.VMEM((angles, 4, window, block), jnp.float32)] * 3
            + [pltpu.VMEM((planes, window, block), jnp.float32)] * 2,
            name=f"slab{slab}",
        )(meta, detuning, *received, *starts)
        exits.append(fields)
        if slab + 1 < sections:
            starts = [fields, from_neighbour(fields, 0, 0), from_neighbour(fields, 1, 0)]

    pieces = {}
    for shift in range(sections):
        mine = pick(lax.rem(depth + shift, sections), exits)
        for turn in range(cores):
            piece = mine[turn]
            pieces[shift, turn] = piece if shift == 0 and turn == 0 else route(piece, shift, turn)
    tiles = []
    for c in range(cores):
        for d in range(sections):
            by_turn = []
            for turn in range(cores):
                by_turn.append(pick(lax.rem(depth - d + sections, sections), [pieces[s, turn] for s in range(sections)]))
            tiles.append(pick(lax.rem(core - c + cores, cores), by_turn))
    return jnp.concatenate(tiles, axis=2)[None, :, None]


def solution(mesh):
    placed = (
        P(None, ("groups", "lat"), None),
        P("depth", ("groups", "lat"), "rock"),
        P(("groups", "rock")),
    )
    return jax.shard_map(
        on_device,
        mesh=mesh,
        in_specs=placed,
        out_specs=P("depth", None, "rock", ("groups", "lat"), None),
        check_vma=False,
    )
```

time: 50.3 us -> 31.5 us (0.63)
  the two profiles are of different devices: /device:TPU:18 before, /device:TPU:0 now
where the time goes in v1:
time: 31.5 us; the launch traced here: 31.2 us
  starting transfers between devices  13.3 us (42%)
  Pallas kernels  6.46 us (21%)
  waiting for transfers between devices  5.26 us (17%)
  other arithmetic  2.82 us (9%)
  local copies, waits for them, and re-layouts  2.55 us (8%)
  between operations  0.75 us (2%)
    ppermute x6, starting transfers between devices, from_neighbour(): lax.ppermute(value, everyone, neighbours(lat, sections, cores, parity, sh...  8.43 us
    ppermute x5, starting transfers between devices, route(): return lax.ppermute(value, ('depth', 'rock'), pairs)  4.89 us
    pallas_call x2, Pallas kernels, on_device(): pl.pallas_call(functools.partial(slab_kernel, sections=sections, slab=sla...  4.79 us
    ppermute x5, waiting for transfers between devices, route(): return lax.ppermute(value, ('depth', 'rock'), pairs)  2.8 us
    ppermute x6, waiting for transfers between devices, from_neighbour(): lax.ppermute(value, everyone, neighbours(lat, sections, cores, parity, sh...  2.46 us
    unnamed x16, local copies, waits for them, and re-layouts  1.88 us
    pallas_call x1, Pallas kernels, on_device(): pl.pallas_call(functools.partial(pack_kernel, sections=sections), out_sha...  1.67 us
    concatenate x1, other arithmetic, on_device(): detuning = jnp.concatenate(detuning)  1.29 us
  transfers between devices with their start and end apart: 11, of which 4 were waited for; matrix products, arithmetic and copies ran while one was open for 4% of the time, Pallas kernels for 0%

profile of v1, /device:TPU:0, one launch (start us, length us, event | category | flops | bytes accessed | tf_op | source)
XLA Modules:
  0.0 31.2 jit_solution(16740431068311281005)
XLA Ops:
  0.0 0.7 %stack.31.meta = s32[5]{0:T(128)} concatenate(s32[1]{0:T(128)} %bitcast, s32[1]{0:T(128)} %bitcast.1, s32[1]{0:T(128)} %bitcast.2, s32[1]{0:T(128)} %bitcast.3, s32[1]{0:T(128)} %bitcast.4), dimensions={0} | concatenate | bytes 40 | tf_op jit(solution)/shard_map/stack | solution.py:222
  0.7 1.7 %pack.1 = (f32[8,16,128]{2,1,0:T(8,128)}, f32[2,16,128]{2,1,0:T(8,128)}, f32[6,16,128]{2,1,0:T(8,128)}, f32[6,16,128]{2,1,0:T(8,128)}, f32[8,16,128]{2,1,0:T(8,1...) custom-call(s32[5]{0:T(128)} %stack.31.meta, f32[8,16,256]{2,1,0:T(8,128)} %phase.1, f32[2,16,512]{2,1,0:T(8,128)} %incident.1), custom_call_target="tpu_custom_call" | custom-call | tf_op jit(solution)/shard_map/pack/pallas_call | solution.py:228
  2.3 3.0 %collective-permute-start.3 = (f32[8,16,128]{2,1,0:T(8,128)}, f32[8,16,128]{2,1,0:T(8,128)S(1)}, u32[]{:S(2)}, u32[]{:S(2)}) collective-permute-start(f32[8,16,128]{2,1,0:T(8,128)} %get-tuple-element.15), channel_id=1, source_target_pairs={{0,2},{1,3},{2,0},{3,1},{4,6},{5,7},{6,4},{7,5},{8,10},{9,11},{10,... | collective-permute-start | bytes 196616 | tf_op jit(solution)/shard_map/ppermute | solution.py:220
  5.3 1.6 %collective-permute-start.1 = (f32[6,16,128]{2,1,0:T(8,128)}, f32[6,16,128]{2,1,0:T(8,128)S(1)}, u32[]{:S(2)}, u32[]{:S(2)}) collective-permute-start(f32[6,16,128]{2,1,0:T(8,128)} %get-tuple-element.13), channel_id=1, source_target_pairs={{0,4},{1,5},{2,6},{3,7},{4,0},{5,1},{6,2},{7,3},{8,12},{9,13},{10,... | collective-permute-start | bytes 147464 | tf_op jit(solution)/shard_map/ppermute | solution.py:213
  6.9 3.1 %collective-permute-start.4 = (f32[4,16,128]{2,1,0:T(8,128)}, f32[4,16,128]{2,1,0:T(8,128)S(1)}, u32[]{:S(2)}, u32[]{:S(2)}) collective-permute-start(f32[4,16,128]{2,1,0:T(8,128)} %get-tuple-element.16), channel_id=1, source_target_pairs={{0,6},{1,7},{2,4},{3,5},{4,2},{5,3},{6,0},{7,1},{8,14},{9,15},{10,... | collective-permute-start | bytes 98312 | tf_op jit(solution)/shard_map/ppermute | solution.py:213
  10.6 0.6 %collective-permute-done = f32[1]{0:T(128)} collective-permute-done((f32[1]{0:T(128)}, f32[1]{0:T(128)}, u32[]{:S(2)}, u32[]{:S(2)}) %collective-permute-start) | collective-permute-done | bytes 36 | tf_op jit(solution)/shard_map/ppermute | solution.py:220
  11.3 0.2 collective-permute-start.5
  11.5 1.3 %pad_maximum_fusion.detuning = f32[2]{0:T(128)} fusion(f32[1]{0:T(128)} %collective-permute-done, f32[1]{0:T(128)S(6)} %copy.5), kind=kLoop, calls=%fused_computation.15 | loop fusion | flops 2 | bytes 16 | tf_op jit(solution)/shard_map/concatenate | solution.py:239
  12.8 0.5 %copy-done.4 = f32[4,16,128]{2,1,0:T(8,128)} copy-done((f32[4,16,128]{2,1,0:T(8,128)}, f32[4,16,128]{2,1,0:T(8,128)S(1)}, u32[]{:S(2)}) %copy-start.4) | copy-done | bytes 32792
  13.4 0.0 copy-done.1
  13.4 0.0 copy-done.3
  13.5 2.4 %slab0.1.refs_6_ = f32[2,4,16,128]{3,2,1,0:T(8,128)} custom-call(s32[5]{0:T(128)} %stack.31.meta, f32[2]{0:T(128)} %pad_maximum_fusion.detuning, f32[8,16,128]{2,1,0:T(8,128)} %get-tuple-element.12.refs_0_, f32[6,16,128]{2,1,0:T(8,128)} %copy-done.1, f32[6,16,128]{2,1,0:T(8,128)} %copy-done.2, f32[8,16,128]{2,1,0:T(8,128)} %copy-done.3, ...), custom_call_target="tpu_custom_call" | custom-call | tf_op jit(solution)/shard_map/slab0/pallas_call | solution.py:249
  15.8 3.5 %collective-permute-start.6 = (f32[2,4,16,128]{3,2,1,0:T(8,128)}, f32[2,4,16,128]{3,2,1,0:T(8,128)S(1)}, u32[]{:S(2)}, u32[]{:S(2)}) collective-permute-start(f32[2,4,16,128]{3,2,1,0:T(8,128)} %slab0.1.refs_6_), channel_id=1, source_target_pairs={{0,4},{1,5},{2,6},{3,7},{4,0},{5,1},{6,2},{7,3},{8,12},{9,13},{10,... | collective-permute-start | bytes 196616 | tf_op jit(solution)/shard_map/ppermute | solution.py:213
  19.4 2.4 %collective-permute-done.6.refs_7_ = f32[2,4,16,128]{3,2,1,0:T(8,128)S(1)} collective-permute-done((f32[2,4,16,128]{3,2,1,0:T(8,128)}, f32[2,4,16,128]{3,2,1,0:T(8,128)S(1)}, u32[]{:S(2)}, u32[]{:S(2)}) %collective-permute-start.6) | collective-permute-done | bytes 65568 | tf_op jit(solution)/shard_map/ppermute | solution.py:213
  21.8 0.6 %copy-done.6 = f32[2,4,16,128]{3,2,1,0:T(8,128)} copy-done((f32[2,4,16,128]{3,2,1,0:T(8,128)}, f32[2,4,16,128]{3,2,1,0:T(8,128)S(1)}, u32[]{:S(2)}) %copy-start.6) | copy-done | bytes 65560
  22.4 0.6 %copy-done.7 = f32[2,4,16,128]{3,2,1,0:T(8,128)} copy-done((f32[2,4,16,128]{3,2,1,0:T(8,128)}, f32[2,4,16,128]{3,2,1,0:T(8,128)S(1)}, u32[]{:S(2)}) %copy-start.7) | copy-done | bytes 65560
  23.1 2.4 %slab1.1 = f32[2,4,16,128]{3,2,1,0:T(8,128)} custom-call(s32[5]{0:T(128)} %stack.31.meta, f32[2]{0:T(128)} %pad_maximum_fusion.detuning, f32[8,16,128]{2,1,0:T(8,128)} %get-tuple-element.12.refs_0_, f32[6,16,128]{2,1,0:T(8,128)} %copy-done.1, f32[6,16,128]{2,1,0:T(8,128)} %copy-done.2, f32[8,16,128]{2,1,0:T(8,128)} %copy-done.3, f32[4,16,128]{2,1,0:T(8,128)} %copy-done.4, ...), custom_call_target="tpu_custom_call" | custom-call | tf_op jit(solution)/shard_map/slab1/pallas_call | solution.py:249
  25.5 0.9 %broadcast_select_fusion = (f32[2,4,16,128]{3,2,1,0:T(8,128)S(1)}, f32[2,4,16,128]{3,2,1,0:T(8,128)S(1)}) fusion(f32[2,4,16,128]{3,2,1,0:T(8,128)S(1)} %copy-done, f32[2,4,16,128]{3,2,1,0:T(8,128)} %slab1.1, pred[]{:T(512)S(6)} %eq.15, pred[]{:T(512)S(6)} %eq.14), kind=kLoop, calls=%fused_computation.5 | loop fusion | flops 32768 | bytes 262146 | tf_op jit(solution)/shard_map/jit(_where)/select_n | solution.py:51
  26.4 0.1 collective-permute-start.10
  26.4 0.6 %collective-permute-start.8 = (f32[4,16,128]{2,1,0:T(8,128)S(1)}, f32[4,16,128]{2,1,0:T(8,128)S(1)}, u32[]{:S(2)}, u32[]{:S(2)}) collective-permute-start(f32[4,16,128]{2,1,0:T(8,128)S(1)} %get-tuple-element.25), channel_id=1, source_target_pairs={{0,2},{1,3},{2,0},{3,1},{4,6},{5,7},{6,4},{7,5},{8,10},{9,11},{10,... | collective-permute-start | bytes 98312 | tf_op jit(solution)/shard_map/ppermute | solution.py:220
  27.1 1.2 %collective-permute-start.9 = (f32[4,16,128]{2,1,0:T(8,128)S(1)}, f32[4,16,128]{2,1,0:T(8,128)S(1)}, u32[]{:S(2)}, u32[]{:S(2)}) collective-permute-start(f32[4,16,128]{2,1,0:T(8,128)S(1)} %slice_bitcast_fusion.1), channel_id=1, source_target_pairs={{0,1},{1,0},{2,3},{3,2},{4,5},{5,4},{6,7},{7,6},{8,9},{9,8},{10,11... | collective-permute-start | bytes 98312 | tf_op jit(solution)/shard_map/ppermute | solution.py:220
  28.3 1.5 %collective-permute-done.10 = f32[4,16,128]{2,1,0:T(8,128)S(1)} collective-permute-done((f32[4,16,128]{2,1,0:T(8,128)S(1)}, f32[4,16,128]{2,1,0:T(8,128)S(1)}, u32[]{:S(2)}, u32[]{:S(2)}) %collective-permute-start.10) | collective-permute-done | bytes 32800 | tf_op jit(solution)/shard_map/ppermute | solution.py:220
  29.8 0.7 %collective-permute-done.8 = f32[4,16,128]{2,1,0:T(8,128)S(1)} collective-permute-done((f32[4,16,128]{2,1,0:T(8,128)S(1)}, f32[4,16,128]{2,1,0:T(8,128)S(1)}, u32[]{:S(2)}, u32[]{:S(2)}) %collective-permute-start.8) | collective-permute-done | bytes 32800 | tf_op jit(solution)/shard_map/ppermute | solution.py:220
  30.5 0.7 %maximum_bitcast_fusion = f32[1,4,1,16,512]{4,3,2,1,0:T(8,128)} fusion(f32[4,16,128]{2,1,0:T(8,128)S(1)} %get-tuple-element.20, f32[4,16,128]{2,1,0:T(8,128)S(1)} %get-tuple-element.21, f32[4,16,128]{2,1,0:T(8,128)S(1)} %get-tuple-element.22, f32[4,16,128]{2,1,0:T(8,128)S(1)} %get-tuple-element.19), kind=kLoop, calls=%fused_computation | loop fusion | flops 98304 | bytes 262144 | tf_op jit(solution)/shard_map/broadcast_in_dim | solution.py:275
  (24 shorter events, 0.1 us)
Async XLA Ops:
  2.3 10.5 %collective-permute-start.3 = (f32[8,16,128]{2,1,0:T(8,128)}, f32[8,16,128]{2,1,0:T(8,128)S(1)}, u32[]{:S(2)}, u32[]{:S(2)}) collective-permute-start(f32[8,16,128]{2,1,0:T(8,128)} %get-tuple-element.15), channel_id=1, source_target_pairs={{0,2},{1,3},{2,0},{3,1},{4,6},{5,7},{6,4},{7,5},{8,10},{9,11},{10,... | collective-permute-start | bytes 196616 | tf_op jit(solution)/shard_map/ppermute | solution.py:220
  5.3 7.5 %collective-permute-start.1 = (f32[6,16,128]{2,1,0:T(8,128)}, f32[6,16,128]{2,1,0:T(8,128)S(1)}, u32[]{:S(2)}, u32[]{:S(2)}) collective-permute-start(f32[6,16,128]{2,1,0:T(8,128)} %get-tuple-element.13), channel_id=1, source_target_pairs={{0,4},{1,5},{2,6},{3,7},{4,0},{5,1},{6,2},{7,3},{8,12},{9,13},{10,... | collective-permute-start | bytes 147464 | tf_op jit(solution)/shard_map/ppermute | solution.py:213
  6.9 5.9 %collective-permute-start.2 = (f32[6,16,128]{2,1,0:T(8,128)}, f32[6,16,128]{2,1,0:T(8,128)S(1)}, u32[]{:S(2)}, u32[]{:S(2)}) collective-permute-start(f32[6,16,128]{2,1,0:T(8,128)} %get-tuple-element.14), channel_id=1, source_target_pairs={{0,1},{1,0},{2,3},{3,2},{4,8},{5,9},{6,10},{7,11},{8,4},{9,5},{10,... | collective-permute-start | bytes 147464 | tf_op jit(solution)/shard_map/ppermute | solution.py:213
  6.9 5.9 %collective-permute-start.4 = (f32[4,16,128]{2,1,0:T(8,128)}, f32[4,16,128]{2,1,0:T(8,128)S(1)}, u32[]{:S(2)}, u32[]{:S(2)}) collective-permute-start(f32[4,16,128]{2,1,0:T(8,128)} %get-tuple-element.16), channel_id=1, source_target_pairs={{0,6},{1,7},{2,4},{3,5},{4,2},{5,3},{6,0},{7,1},{8,14},{9,15},{10,... | collective-permute-start | bytes 98312 | tf_op jit(solution)/shard_map/ppermute | solution.py:213
  10.0 1.3 %collective-permute-start = (f32[1]{0:T(128)}, f32[1]{0:T(128)}, u32[]{:S(2)}, u32[]{:S(2)}) collective-permute-start(f32[1]{0:T(128)} %param.5), channel_id=1, source_target_pairs={{0,1},{1,0},{2,3},{3,2},{4,5},{5,4},{6,7},{7,6},{8,9},{9,8},{10,11... | collective-permute-start | bytes 20 | tf_op jit(solution)/shard_map/ppermute | solution.py:220
  11.3 1.5 %collective-permute-start.5 = (f32[4,16,128]{2,1,0:T(8,128)}, f32[4,16,128]{2,1,0:T(8,128)S(1)}, u32[]{:S(2)}, u32[]{:S(2)}) collective-permute-start(f32[4,16,128]{2,1,0:T(8,128)} %get-tuple-element.17), channel_id=1, source_target_pairs={{0,1},{1,0},{2,3},{3,2},{4,10},{5,11},{6,8},{7,9},{8,6},{9,7},{10,... | collective-permute-start | bytes 98312 | tf_op jit(solution)/shard_map/ppermute | solution.py:213
  12.8 0.6 %copy-start.4 = (f32[4,16,128]{2,1,0:T(8,128)}, f32[4,16,128]{2,1,0:T(8,128)S(1)}, u32[]{:S(2)}) copy-start(f32[4,16,128]{2,1,0:T(8,128)S(1)} %collective-permute-done.4.refs_4_) | copy-start | bytes 98308
  12.8 0.6 %copy-start.5 = (f32[4,16,128]{2,1,0:T(8,128)}, f32[4,16,128]{2,1,0:T(8,128)S(1)}, u32[]{:S(2)}) copy-start(f32[4,16,128]{2,1,0:T(8,128)S(1)} %collective-permute-done.5.refs_5_) | copy-start | bytes 98308
  12.8 0.6 %copy-start.1 = (f32[6,16,128]{2,1,0:T(8,128)}, f32[6,16,128]{2,1,0:T(8,128)S(1)}, u32[]{:S(2)}) copy-start(f32[6,16,128]{2,1,0:T(8,128)S(1)} %collective-permute-done.1.refs_1_.refs_7_) | copy-start | bytes 147460
  12.8 0.6 %copy-start.2 = (f32[6,16,128]{2,1,0:T(8,128)}, f32[6,16,128]{2,1,0:T(8,128)S(1)}, u32[]{:S(2)}) copy-start(f32[6,16,128]{2,1,0:T(8,128)S(1)} %collective-permute-done.2.refs_2_.refs_8_) | copy-start | bytes 147460
  12.8 0.6 %copy-start.3 = (f32[8,16,128]{2,1,0:T(8,128)}, f32[8,16,128]{2,1,0:T(8,128)S(1)}, u32[]{:S(2)}) copy-start(f32[8,16,128]{2,1,0:T(8,128)S(1)} %collective-permute-done.3.refs_3_) | copy-start | bytes 196612
  15.8 6.0 %collective-permute-start.6 = (f32[2,4,16,128]{3,2,1,0:T(8,128)}, f32[2,4,16,128]{3,2,1,0:T(8,128)S(1)}, u32[]{:S(2)}, u32[]{:S(2)}) collective-permute-start(f32[2,4,16,128]{3,2,1,0:T(8,128)} %slab0.1.refs_6_), channel_id=1, source_target_pairs={{0,4},{1,5},{2,6},{3,7},{4,0},{5,1},{6,2},{7,3},{8,12},{9,13},{10,... | collective-permute-start | bytes 196616 | tf_op jit(solution)/shard_map/ppermute | solution.py:213
  19.4 2.5 %collective-permute-start.7 = (f32[2,4,16,128]{3,2,1,0:T(8,128)}, f32[2,4,16,128]{3,2,1,0:T(8,128)S(1)}, u32[]{:S(2)}, u32[]{:S(2)}) collective-permute-start(f32[2,4,16,128]{3,2,1,0:T(8,128)} %slab0.1.refs_6_), channel_id=1, source_target_pairs={{0,1},{1,0},{2,3},{3,2},{4,8},{5,9},{6,10},{7,11},{8,4},{9,5},{10,... | collective-permute-start | bytes 196616 | tf_op jit(solution)/shard_map/ppermute | solution.py:213
  19.4 6.1 %copy-start = (f32[2,4,16,128]{3,2,1,0:T(8,128)S(1)}, f32[2,4,16,128]{3,2,1,0:T(8,128)}, u32[]{:S(2)}) copy-start(f32[2,4,16,128]{3,2,1,0:T(8,128)} %slab0.1.refs_6_) | copy-start | bytes 196612
  21.8 0.6 %copy-start.6 = (f32[2,4,16,128]{3,2,1,0:T(8,128)}, f32[2,4,16,128]{3,2,1,0:T(8,128)S(1)}, u32[]{:S(2)}) copy-start(f32[2,4,16,128]{3,2,1,0:T(8,128)S(1)} %collective-permute-done.6.refs_7_) | copy-start | bytes 196612
  22.4 0.6 %copy-start.7 = (f32[2,4,16,128]{3,2,1,0:T(8,128)}, f32[2,4,16,128]{3,2,1,0:T(8,128)S(1)}, u32[]{:S(2)}) copy-start(f32[2,4,16,128]{3,2,1,0:T(8,128)S(1)} %collective-permute-done.7.refs_8_) | copy-start | bytes 196612
  26.4 3.4 %collective-permute-start.10 = (f32[4,16,128]{2,1,0:T(8,128)S(1)}, f32[4,16,128]{2,1,0:T(8,128)S(1)}, u32[]{:S(2)}, u32[]{:S(2)}) collective-permute-start(f32[4,16,128]{2,1,0:T(8,128)S(1)} %get-tuple-element.26), channel_id=1, source_target_pairs={{0,3},{1,2},{2,1},{3,0},{4,7},{5,6},{6,5},{7,4},{8,11},{9,10},{10,... | collective-permute-start | bytes 98312 | tf_op jit(solution)/shard_map/ppermute | solution.py:220
  26.4 4.0 %collective-permute-start.8 = (f32[4,16,128]{2,1,0:T(8,128)S(1)}, f32[4,16,128]{2,1,0:T(8,128)S(1)}, u32[]{:S(2)}, u32[]{:S(2)}) collective-permute-start(f32[4,16,128]{2,1,0:T(8,128)S(1)} %get-tuple-element.25), channel_id=1, source_target_pairs={{0,2},{1,3},{2,0},{3,1},{4,6},{5,7},{6,4},{7,5},{8,10},{9,11},{10,... | collective-permute-start | bytes 98312 | tf_op jit(solution)/shard_map/ppermute | solution.py:220
  27.1 3.4 %collective-permute-start.9 = (f32[4,16,128]{2,1,0:T(8,128)S(1)}, f32[4,16,128]{2,1,0:T(8,128)S(1)}, u32[]{:S(2)}, u32[]{:S(2)}) collective-permute-start(f32[4,16,128]{2,1,0:T(8,128)S(1)} %slice_bitcast_fusion.1), channel_id=1, source_target_pairs={{0,1},{1,0},{2,3},{3,2},{4,5},{5,4},{6,7},{7,6},{8,9},{9,8},{10,11... | collective-permute-start | bytes 98312 | tf_op jit(solution)/shard_map/ppermute | solution.py:220

commit v2 on v1

--- a/solution.py
+++ b/solution.py
@@ -58,12 +58,20 @@
     return pick(index, [ref[:, :, i * block : (i + 1) * block] for i in range(count)])
 
 
-def pack_kernel(meta, phase, incident, *outs, sections):
+def position():
+    row = lax.axis_index("lat")
+    return lax.axis_index("depth"), lax.rem(row, 2), row > 0, row + 1 < lax.axis_size("lat")
+
+
+def pack_kernel(detuning, phase, incident, *outs, sections):
     planes, rows, block = outs[0].shape
     width = 2 * planes
-    own, entrance, sends = outs[0], outs[1], outs[2:]
-    depth, odd = meta[0], meta[1]
-    entrance[...] = columns_at(incident, meta[4] * sections + depth, incident.shape[2] // block, block)
+    own, entrance, turns, sends = outs[0], outs[1], outs[2], outs[3:]
+    depth, odd, _, _ = position()
+    for a in range(turns.shape[0]):
+        turns[a] = jnp.full(turns.shape[1:], detuning[a] * (1.0 / nu))
+    which = lax.axis_index("rock") * sections + depth
+    entrance[...] = columns_at(incident, which, incident.shape[2] // block, block)
     for shift in range(sections):
         target = lax.rem(depth + shift, sections)
         if shift == 0:
@@ -95,10 +103,11 @@
             fill(odd_pairs, even_pairs)
 
 
-def slab_kernel(meta, detuning, *refs, sections, slab, planes, rows):
+def slab_kernel(*refs, sections, slab, cores, planes, rows):
     width = 2 * planes
-    odd, lower, upper = meta[1], meta[2] > 0, meta[3] > 0
-    source = lax.rem(meta[0] - slab + sections, sections)
+    depth, odd, lower, upper = position()
+    source = lax.rem(depth - slab + sections, sections)
+    turn_refs, refs = refs[:cores], refs[cores:]
     phases, refs = refs[: 3 * sections], refs[3 * sections :]
     starts, refs = refs[:3], refs[3:]
     out, v0, v1, w, cs, ss = refs
@@ -158,7 +167,7 @@
             (stay * bi + bi_next) + (cosine * tr + sine * ti) + turn * br,
         )
 
-    turns = [detuning[a] * (1.0 / nu) for a in range(angles)]
+    turns = [ref[a] for ref in turn_refs for a in range(ref.shape[0])]
     now, later = v0, v1
     for p in range(planes):
         reach = 2 * (planes - p) - 1
@@ -182,6 +191,7 @@
 
 VMEM = pl.BlockSpec(memory_space=pltpu.VMEM)
 SMEM = pl.BlockSpec(memory_space=pltpu.SMEM)
+GRANT = pltpu.CompilerParams(vmem_limit_bytes=16 * 2**20)
 
 
 def neighbours(lat, sections, cores, parity, shift):
@@ -219,9 +229,8 @@
                 pairs.append((d * cores + c, (d + shift) % sections * cores + (c + turn) % cores))
         return lax.ppermute(value, ("depth", "rock"), pairs)
 
-    meta = jnp.stack([depth, row % 2, row > 0, row + 1 < lat, core]).astype(jnp.int32)
     shape = lambda *dims: jax.ShapeDtypeStruct(dims, jnp.float32)
-    outs = [shape(planes, rows, block), shape(2, rows, block)]
+    outs = [shape(planes, rows, block), shape(2, rows, block), shape(deviation.shape[0], 8, block)]
     outs += [shape(planes // 2 + 2, width, block)] * 2
     for _ in range(1, sections):
         outs += [shape(planes, rows, block)] + [shape(planes // 2, width, block)] * 2
@@ -230,13 +239,11 @@
         out_shape=outs,
         in_specs=[SMEM, VMEM, VMEM],
         out_specs=[VMEM] * len(outs),
+        compiler_params=GRANT,
         name="pack",
-    )(meta, phase, incident)
-    own, entrance, sends = packed[0], packed[1], packed[2:]
-    detuning = [deviation]
-    for turn in range(1, cores):
-        detuning.append(route(deviation, 0, turn))
-    detuning = jnp.concatenate(detuning)
+    )(deviation, phase, incident)
+    own, entrance, turns, sends = packed[0], packed[1], packed[2], packed[3:]
+    turns = [turns] + [route(turns, 0, turn) for turn in range(1, cores)]
     received = [own, from_neighbour(sends[0], 0, 0), from_neighbour(sends[1], 1, 0)]
     for shift in range(1, sections):
         full, even, odd = sends[3 * shift - 1 : 3 * shift + 2]
@@ -247,14 +254,15 @@
     window = rows + 2 * width + 16
     for slab in range(sections):
         fields = pl.pallas_call(
-            functools.partial(slab_kernel, sections=sections, slab=slab, planes=planes, rows=rows),
+            functools.partial(slab_kernel, sections=sections, slab=slab, cores=cores, planes=planes, rows=rows),
             out_shape=shape(angles, 4, rows, block),
-            in_specs=[SMEM, SMEM] + [VMEM] * (len(received) + 3),
+            in_specs=[VMEM] * (cores + len(received) + 3),
             out_specs=VMEM,
             scratch_shapes=[pltpu.VMEM((angles, 4, window, block), jnp.float32)] * 3
             + [pltpu.VMEM((planes, window, block), jnp.float32)] * 2,
+            compiler_params=GRANT,
             name=f"slab{slab}",
-        )(meta, detuning, *received, *starts)
+        )(*turns, *received, *starts)
         exits.append(fields)
         if slab + 1 < sections:
             starts = [fields, from_neighbour(fields, 0, 0), from_neighbour(fields, 1, 0)]

time: 31.5 us -> 25 us (0.79)
  Pallas kernels: 6.46 us -> 1.53 us
  other arithmetic: 2.82 us -> 0.69 us
  waiting for transfers between devices: 5.26 us -> 6.4 us
  local copies, waits for them, and re-layouts: 2.55 us -> 1.75 us
  starting transfers between devices: 13.3 us -> 13.7 us
    pallas_call x2, Pallas kernels: 4.79 us -> 1.5 us  [on_device(): pl.pallas_call(functools.partial(slab_kernel, sections=sections, slab=sla...]
    ppermute x6, waiting for transfers between devices: 2.46 us -> 4.22 us  [from_neighbour(): lax.ppermute(value, everyone, neighbours(lat, sections, cores, parity, sh...]
    pallas_call x1, Pallas kernels: 1.67 us -> 0.04 us  [on_device(): pl.pallas_call(functools.partial(pack_kernel, sections=sections), out_sha...]
    concatenate x1 -> x0, other arithmetic: 1.29 us -> none  [on_device(): detuning = jnp.concatenate(detuning)]
    select_n x2, other arithmetic: 0.86 us -> 0.03 us  [pick(): out = jnp.where(index == i, values[i], out)]
    another operation x1 -> x0, local copies, waits for them, and re-layouts: 0.66 us -> none  [on_device(): jnp.stack([depth, row % 2, row > 0, row + 1 < lat, core]).astype(jnp.int32)]
    ppermute x5, waiting for transfers between devices: 2.8 us -> 2.18 us  [route(): return lax.ppermute(value, ('depth', 'rock'), pairs)]
    ppermute x5, starting transfers between devices: 4.89 us -> 5.46 us  [route(): return lax.ppermute(value, ('depth', 'rock'), pairs)]
  transfers between devices with their start and end apart: 11 -> 11, of which waited for: 4 -> 4; matrix products, arithmetic and copies ran while one was open for 4% -> 0% of each run, Pallas kernels for 0% -> 0%
where the time goes in v2:
time: 25 us; the launch traced here: 24.9 us
  starting transfers between devices  13.7 us (55%)
  waiting for transfers between devices  6.4 us (26%)
  local copies, waits for them, and re-layouts  1.75 us (7%)
  Pallas kernels  1.53 us (6%)
  between operations  0.74 us (3%)
  other arithmetic  0.69 us (3%)
    ppermute x6, starting transfers between devices, from_neighbour(): lax.ppermute(value, everyone, neighbours(lat, sections, cores, parity, sh...  8.28 us
    ppermute x5, starting transfers between devices, route(): return lax.ppermute(value, ('depth', 'rock'), pairs)  5.46 us
    ppermute x6, waiting for transfers between devices, from_neighbour(): lax.ppermute(value, everyone, neighbours(lat, sections, cores, parity, sh...  4.22 us
    ppermute x5, waiting for transfers between devices, route(): return lax.ppermute(value, ('depth', 'rock'), pairs)  2.18 us
    unnamed x4, local copies, waits for them, and re-layouts  1.74 us
    pallas_call x2, Pallas kernels, on_device(): pl.pallas_call(functools.partial(slab_kernel, sections=sections, slab=sla...  1.5 us
    broadcast_in_dim x1, other arithmetic, on_device(): return jnp.concatenate(tiles, axis=2)[None, :, None]  0.67 us
  transfers between devices with their start and end apart: 11, of which 4 were waited for; matrix products, arithmetic and copies ran while one was open for 0% of the time, Pallas kernels for 0%

profile of v2, /device:TPU:0, one launch (start us, length us, event | category | flops | bytes accessed | tf_op | source)
XLA Modules:
  0.0 24.9 jit_solution(12183007773772854255)
XLA Ops:
  0.7 0.9 %copy-done = f32[8,16,256]{2,1,0:T(8,128)S(1)} copy-done((f32[8,16,256]{2,1,0:T(8,128)S(1)}, f32[8,16,256]{2,1,0:T(8,128)}, u32[]{:S(2)}) %copy-start) | copy-done | bytes 131096
  1.6 0.8 %copy-done.1 = f32[2,16,512]{2,1,0:T(8,128)S(1)} copy-done((f32[2,16,512]{2,1,0:T(8,128)S(1)}, f32[2,16,512]{2,1,0:T(8,128)}, u32[]{:S(2)}) %copy-start.1) | copy-done | bytes 65560
  2.4 3.0 %collective-permute-start.3 = (f32[8,16,128]{2,1,0:T(8,128)S(1)}, f32[8,16,128]{2,1,0:T(8,128)S(1)}, u32[]{:S(2)}, u32[]{:S(2)}) collective-permute-start(f32[8,16,128]{2,1,0:T(8,128)S(1)} %get-tuple-element.17), channel_id=1, source_target_pairs={{0,2},{1,3},{2,0},{3,1},{4,6},{5,7},{6,4},{7,5},{8,10},{9,11},{10,... | collective-permute-start | bytes 196616 | tf_op jit(solution)/shard_map/ppermute | solution.py:230
  5.5 1.6 %collective-permute-start.1 = (f32[6,16,128]{2,1,0:T(8,128)S(1)}, f32[6,16,128]{2,1,0:T(8,128)S(1)}, u32[]{:S(2)}, u32[]{:S(2)}) collective-permute-start(f32[6,16,128]{2,1,0:T(8,128)S(1)} %get-tuple-element.15), channel_id=1, source_target_pairs={{0,4},{1,5},{2,6},{3,7},{4,0},{5,1},{6,2},{7,3},{8,12},{9,13},{10,... | collective-permute-start | bytes 147464 | tf_op jit(solution)/shard_map/ppermute | solution.py:223
  7.0 0.0 collective-permute-start.2
  7.0 0.5 %collective-permute-start = (f32[1,8,128]{2,1,0:T(8,128)S(1)}, f32[1,8,128]{2,1,0:T(8,128)S(1)}, u32[]{:S(2)}, u32[]{:S(2)}) collective-permute-start(f32[1,8,128]{2,1,0:T(8,128)S(1)} %get-tuple-element.13.refs_0_), channel_id=1, source_target_pairs={{0,1},{1,0},{2,3},{3,2},{4,5},{5,4},{6,7},{7,6},{8,9},{9,8},{10,11... | collective-permute-start | bytes 12296 | tf_op jit(solution)/shard_map/ppermute | solution.py:230
  7.6 2.6 %collective-permute-start.4 = (f32[4,16,128]{2,1,0:T(8,128)S(1)}, f32[4,16,128]{2,1,0:T(8,128)S(1)}, u32[]{:S(2)}, u32[]{:S(2)}) collective-permute-start(f32[4,16,128]{2,1,0:T(8,128)S(1)} %get-tuple-element.18), channel_id=1, source_target_pairs={{0,6},{1,7},{2,4},{3,5},{4,2},{5,3},{6,0},{7,1},{8,14},{9,15},{10,... | collective-permute-start | bytes 98312 | tf_op jit(solution)/shard_map/ppermute | solution.py:223
  10.2 0.0 collective-permute-done.refs_1_
  10.2 0.2 collective-permute-start.5
  10.4 2.0 %collective-permute-done.4.refs_6_ = f32[4,16,128]{2,1,0:T(8,128)S(1)} collective-permute-done((f32[4,16,128]{2,1,0:T(8,128)S(1)}, f32[4,16,128]{2,1,0:T(8,128)S(1)}, u32[]{:S(2)}, u32[]{:S(2)}) %collective-permute-start.4) | collective-permute-done | bytes 32800 | tf_op jit(solution)/shard_map/ppermute | solution.py:223
  12.4 0.0 collective-permute-done.5.refs_7_
  12.4 0.0 collective-permute-done.1.refs_3_.refs_9_
  12.4 0.0 collective-permute-done.2.refs_4_.refs_10_
  12.4 0.8 %slab0.1.refs_8_ = f32[2,4,16,128]{3,2,1,0:T(8,128)S(1)} custom-call(f32[1,8,128]{2,1,0:T(8,128)S(1)} %get-tuple-element.13.refs_0_, f32[1,8,128]{2,1,0:T(8,128)S(1)} %collective-permute-done.refs_1_, f32[8,16,128]{2,1,0:T(8,128)S(1)} %get-tuple-element.14.refs_2_, f32[6,16,128]{2,1,0:T(8,128)S(1)} %collective-permute-done.1.refs_3_.refs_9_, ...), custom_call_target="tpu_custom_call" | custom-call | tf_op jit(solution)/shard_map/slab0/pallas_call | solution.py:256
  13.2 3.9 %collective-permute-start.6 = (f32[2,4,16,128]{3,2,1,0:T(8,128)S(1)}, f32[2,4,16,128]{3,2,1,0:T(8,128)S(1)}, u32[]{:S(2)}, u32[]{:S(2)}) collective-permute-start(f32[2,4,16,128]{3,2,1,0:T(8,128)S(1)} %slab0.1.refs_8_), channel_id=1, source_target_pairs={{0,4},{1,5},{2,6},{3,7},{4,0},{5,1},{6,2},{7,3},{8,12},{9,13},{10,... | collective-permute-start | bytes 196616 | tf_op jit(solution)/shard_map/ppermute | solution.py:223
  17.0 2.2 %collective-permute-done.6.refs_9_ = f32[2,4,16,128]{3,2,1,0:T(8,128)S(1)} collective-permute-done((f32[2,4,16,128]{3,2,1,0:T(8,128)S(1)}, f32[2,4,16,128]{3,2,1,0:T(8,128)S(1)}, u32[]{:S(2)}, u32[]{:S(2)}) %collective-permute-start.6) | collective-permute-done | bytes 65568 | tf_op jit(solution)/shard_map/ppermute | solution.py:223
  19.3 0.0 collective-permute-done.7.refs_10_
  19.3 0.7 %slab1.1 = f32[2,4,16,128]{3,2,1,0:T(8,128)S(1)} custom-call(f32[1,8,128]{2,1,0:T(8,128)S(1)} %get-tuple-element.13.refs_0_, f32[1,8,128]{2,1,0:T(8,128)S(1)} %collective-permute-done.refs_1_, f32[8,16,128]{2,1,0:T(8,128)S(1)} %get-tuple-element.14.refs_2_, f32[6,16,128]{2,1,0:T(8,128)S(1)} %collective-permute-done.1.refs_3_.refs_9_, ...), custom_call_target="tpu_custom_call" | custom-call | tf_op jit(solution)/shard_map/slab1/pallas_call | solution.py:256
  20.1 0.1 collective-permute-start.10
  20.1 0.8 %collective-permute-start.8 = (f32[4,16,128]{2,1,0:T(8,128)S(1)}, f32[4,16,128]{2,1,0:T(8,128)S(1)}, u32[]{:S(2)}, u32[]{:S(2)}) collective-permute-start(f32[4,16,128]{2,1,0:T(8,128)S(1)} %get-tuple-element.27), channel_id=1, source_target_pairs={{0,2},{1,3},{2,0},{3,1},{4,6},{5,7},{6,4},{7,5},{8,10},{9,11},{10,... | collective-permute-start | bytes 98312 | tf_op jit(solution)/shard_map/ppermute | solution.py:230
  20.9 1.1 %collective-permute-start.9 = (f32[4,16,128]{2,1,0:T(8,128)S(1)}, f32[4,16,128]{2,1,0:T(8,128)S(1)}, u32[]{:S(2)}, u32[]{:S(2)}) collective-permute-start(f32[4,16,128]{2,1,0:T(8,128)S(1)} %slice_bitcast_fusion.1), channel_id=1, source_target_pairs={{0,1},{1,0},{2,3},{3,2},{4,5},{5,4},{6,7},{7,6},{8,9},{9,8},{10,11... | collective-permute-start | bytes 98312 | tf_op jit(solution)/shard_map/ppermute | solution.py:230
  22.0 1.5 %collective-permute-done.10 = f32[4,16,128]{2,1,0:T(8,128)S(1)} collective-permute-done((f32[4,16,128]{2,1,0:T(8,128)S(1)}, f32[4,16,128]{2,1,0:T(8,128)S(1)}, u32[]{:S(2)}, u32[]{:S(2)}) %collective-permute-start.10) | collective-permute-done | bytes 32800 | tf_op jit(solution)/shard_map/ppermute | solution.py:230
  23.5 0.7 %collective-permute-done.8 = f32[4,16,128]{2,1,0:T(8,128)S(1)} collective-permute-done((f32[4,16,128]{2,1,0:T(8,128)S(1)}, f32[4,16,128]{2,1,0:T(8,128)S(1)}, u32[]{:S(2)}, u32[]{:S(2)}) %collective-permute-start.8) | collective-permute-done | bytes 32800 | tf_op jit(solution)/shard_map/ppermute | solution.py:230
  24.2 0.7 %maximum_bitcast_fusion = f32[1,4,1,16,512]{4,3,2,1,0:T(8,128)} fusion(f32[4,16,128]{2,1,0:T(8,128)S(1)} %get-tuple-element.22, f32[4,16,128]{2,1,0:T(8,128)S(1)} %get-tuple-element.23, f32[4,16,128]{2,1,0:T(8,128)S(1)} %get-tuple-element.24, f32[4,16,128]{2,1,0:T(8,128)S(1)} %get-tuple-element.21), kind=kLoop, calls=%fused_computation | loop fusion | flops 98304 | bytes 262144 | tf_op jit(solution)/shard_map/broadcast_in_dim | solution.py:283
  (10 shorter events, 0.1 us)
Async XLA Ops:
  0.7 0.9 %copy-start = (f32[8,16,256]{2,1,0:T(8,128)S(1)}, f32[8,16,256]{2,1,0:T(8,128)}, u32[]{:S(2)}) copy-start(f32[8,16,256]{2,1,0:T(8,128)} %phase.1) | copy-start | bytes 393220
  1.6 0.8 %copy-start.1 = (f32[2,16,512]{2,1,0:T(8,128)S(1)}, f32[2,16,512]{2,1,0:T(8,128)}, u32[]{:S(2)}) copy-start(f32[2,16,512]{2,1,0:T(8,128)} %incident.1) | copy-start | bytes 196612
  2.4 9.9 %collective-permute-start.3 = (f32[8,16,128]{2,1,0:T(8,128)S(1)}, f32[8,16,128]{2,1,0:T(8,128)S(1)}, u32[]{:S(2)}, u32[]{:S(2)}) collective-permute-start(f32[8,16,128]{2,1,0:T(8,128)S(1)} %get-tuple-element.17), channel_id=1, source_target_pairs={{0,2},{1,3},{2,0},{3,1},{4,6},{5,7},{6,4},{7,5},{8,10},{9,11},{10,... | collective-permute-start | bytes 196616 | tf_op jit(solution)/shard_map/ppermute | solution.py:230
  5.5 6.9 %collective-permute-start.1 = (f32[6,16,128]{2,1,0:T(8,128)S(1)}, f32[6,16,128]{2,1,0:T(8,128)S(1)}, u32[]{:S(2)}, u32[]{:S(2)}) collective-permute-start(f32[6,16,128]{2,1,0:T(8,128)S(1)} %get-tuple-element.15), channel_id=1, source_target_pairs={{0,4},{1,5},{2,6},{3,7},{4,0},{5,1},{6,2},{7,3},{8,12},{9,13},{10,... | collective-permute-start | bytes 147464 | tf_op jit(solution)/shard_map/ppermute | solution.py:223
  7.0 5.3 %collective-permute-start.2 = (f32[6,16,128]{2,1,0:T(8,128)S(1)}, f32[6,16,128]{2,1,0:T(8,128)S(1)}, u32[]{:S(2)}, u32[]{:S(2)}) collective-permute-start(f32[6,16,128]{2,1,0:T(8,128)S(1)} %get-tuple-element.16), channel_id=1, source_target_pairs={{0,1},{1,0},{2,3},{3,2},{4,8},{5,9},{6,10},{7,11},{8,4},{9,5},{10,... | collective-permute-start | bytes 147464 | tf_op jit(solution)/shard_map/ppermute | solution.py:223
  7.0 3.1 %collective-permute-start = (f32[1,8,128]{2,1,0:T(8,128)S(1)}, f32[1,8,128]{2,1,0:T(8,128)S(1)}, u32[]{:S(2)}, u32[]{:S(2)}) collective-permute-start(f32[1,8,128]{2,1,0:T(8,128)S(1)} %get-tuple-element.13.refs_0_), channel_id=1, source_target_pairs={{0,1},{1,0},{2,3},{3,2},{4,5},{5,4},{6,7},{7,6},{8,9},{9,8},{10,11... | collective-permute-start | bytes 12296 | tf_op jit(solution)/shard_map/ppermute | solution.py:230
  7.6 4.8 %collective-permute-start.4 = (f32[4,16,128]{2,1,0:T(8,128)S(1)}, f32[4,16,128]{2,1,0:T(8,128)S(1)}, u32[]{:S(2)}, u32[]{:S(2)}) collective-permute-start(f32[4,16,128]{2,1,0:T(8,128)S(1)} %get-tuple-element.18), channel_id=1, source_target_pairs={{0,6},{1,7},{2,4},{3,5},{4,2},{5,3},{6,0},{7,1},{8,14},{9,15},{10,... | collective-permute-start | bytes 98312 | tf_op jit(solution)/shard_map/ppermute | solution.py:223
  10.2 2.2 %collective-permute-start.5 = (f32[4,16,128]{2,1,0:T(8,128)S(1)}, f32[4,16,128]{2,1,0:T(8,128)S(1)}, u32[]{:S(2)}, u32[]{:S(2)}) collective-permute-start(f32[4,16,128]{2,1,0:T(8,128)S(1)} %get-tuple-element.19), channel_id=1, source_target_pairs={{0,1},{1,0},{2,3},{3,2},{4,10},{5,11},{6,8},{7,9},{8,6},{9,7},{10,... | collective-permute-start | bytes 98312 | tf_op jit(solution)/shard_map/ppermute | solution.py:223
  13.2 6.1 %collective-permute-start.6 = (f32[2,4,16,128]{3,2,1,0:T(8,128)S(1)}, f32[2,4,16,128]{3,2,1,0:T(8,128)S(1)}, u32[]{:S(2)}, u32[]{:S(2)}) collective-permute-start(f32[2,4,16,128]{3,2,1,0:T(8,128)S(1)} %slab0.1.refs_8_), channel_id=1, source_target_pairs={{0,4},{1,5},{2,6},{3,7},{4,0},{5,1},{6,2},{7,3},{8,12},{9,13},{10,... | collective-permute-start | bytes 196616 | tf_op jit(solution)/shard_map/ppermute | solution.py:223
  17.0 2.2 %collective-permute-start.7 = (f32[2,4,16,128]{3,2,1,0:T(8,128)S(1)}, f32[2,4,16,128]{3,2,1,0:T(8,128)S(1)}, u32[]{:S(2)}, u32[]{:S(2)}) collective-permute-start(f32[2,4,16,128]{3,2,1,0:T(8,128)S(1)} %slab0.1.refs_8_), channel_id=1, source_target_pairs={{0,1},{1,0},{2,3},{3,2},{4,8},{5,9},{6,10},{7,11},{8,4},{9,5},{10,... | collective-permute-start | bytes 196616 | tf_op jit(solution)/shard_map/ppermute | solution.py:223
  20.1 3.4 %collective-permute-start.10 = (f32[4,16,128]{2,1,0:T(8,128)S(1)}, f32[4,16,128]{2,1,0:T(8,128)S(1)}, u32[]{:S(2)}, u32[]{:S(2)}) collective-permute-start(f32[4,16,128]{2,1,0:T(8,128)S(1)} %get-tuple-element.28), channel_id=1, source_target_pairs={{0,3},{1,2},{2,1},{3,0},{4,7},{5,6},{6,5},{7,4},{8,11},{9,10},{10,... | collective-permute-start | bytes 98312 | tf_op jit(solution)/shard_map/ppermute | solution.py:230
  20.1 4.0 %collective-permute-start.8 = (f32[4,16,128]{2,1,0:T(8,128)S(1)}, f32[4,16,128]{2,1,0:T(8,128)S(1)}, u32[]{:S(2)}, u32[]{:S(2)}) collective-permute-start(f32[4,16,128]{2,1,0:T(8,128)S(1)} %get-tuple-element.27), channel_id=1, source_target_pairs={{0,2},{1,3},{2,0},{3,1},{4,6},{5,7},{6,4},{7,5},{8,10},{9,11},{10,... | collective-permute-start | bytes 98312 | tf_op jit(solution)/shard_map/ppermute | solution.py:230
  20.9 3.2 %collective-permute-start.9 = (f32[4,16,128]{2,1,0:T(8,128)S(1)}, f32[4,16,128]{2,1,0:T(8,128)S(1)}, u32[]{:S(2)}, u32[]{:S(2)}) collective-permute-start(f32[4,16,128]{2,1,0:T(8,128)S(1)} %slice_bitcast_fusion.1), channel_id=1, source_target_pairs={{0,1},{1,0},{2,3},{3,2},{4,5},{5,4},{6,7},{7,6},{8,9},{9,8},{10,11... | collective-permute-start | bytes 98312 | tf_op jit(solution)/shard_map/ppermute | solution.py:230

commit v3 on v2

v3 whole, which is shorter than its diff:
```python
import functools
import math

import jax
import jax.numpy as jnp
import numpy as np
from jax import lax
from jax.experimental import pallas as pl
from jax.experimental.pallas import tpu as pltpu
from jax.sharding import PartitionSpec as P

courant = np.float32(0.9)
coupling = np.float32(0.2)


nu = float(courant)
stay = float(np.float32(1.0) - courant) / nu
amplitude = float(coupling) / nu
carry = 1.0 / nu**2


def half_angle_series():
    z = np.linspace(0.0, math.pi**2 * 1.0001, 20001)
    y = np.sqrt(z) / 2
    sine = np.where(y > 0, np.sin(y) / np.maximum(2 * y, 1e-30), 0.5)
    cheb, power = np.polynomial.Chebyshev, np.polynomial.Polynomial
    fits = [cheb.fit(z, v, d).convert(kind=power).coef for v, d in ((sine, 5), (np.cos(y), 6))]
    return [[float(c) for c in fit] for fit in fits]


sine_series, cosine_series = half_angle_series()


def horner(series, z):
    total = series[-1] * z + series[-2]
    for c in series[-3::-1]:
        total = total * z + c
    return total


def scaled_sincos(phi, scale):
    z = phi * phi
    s = horner(sine_series, z) * phi
    t = s * (2.0 * scale)
    return t * horner(cosine_series, z), scale - t * s


def pick(index, values):
    out = values[-1]
    for i in range(len(values) - 2, -1, -1):
        out = jnp.where(index == i, values[i], out)
    return out


def columns_at(ref, index, count, block):
    if block % 128 == 0:
        return ref[:, :, pl.ds(pl.multiple_of(index * block, block), block)]
    return pick(index, [ref[:, :, i * block : (i + 1) * block] for i in range(count)])


def halo_kind(planes, rows, sections, slab, distance):
    need = [2 * ((sections - slab) * planes - p) - 1 - (distance - 1) * rows for p in range(planes)]
    if need[0] <= 0:
        return None
    return "triangle" if planes % 2 == 0 and need[0] == rows - 1 and rows == 2 * planes else "full"


def swaps(lat, sections, cores, distance, parity):
    pairs, real = [], False
    for row in range(lat):
        other = row + distance if row // distance % 2 == parity else row - distance
        real |= 0 <= other < lat
        for depth in range(sections):
            for core in range(cores):
                here = (row * sections + depth) * cores + core
                if 0 <= other < lat:
                    there = (other * sections + depth) * cores + core
                else:
                    there = (row * sections + depth) * cores + (core + 1) % cores
                pairs.append((here, there))
    return pairs if real else None


def columns_kernel(detuning, phase, incident, *outs, sections):
    block = outs[0].shape[2]
    entrance, turns, parts = outs[0], outs[1], outs[2:]
    depth = lax.axis_index("depth")
    for a in range(turns.shape[0]):
        turns[a] = jnp.full(turns.shape[1:], detuning[a] * (1.0 / nu))
    which = lax.axis_index("rock") * sections + depth
    entrance[...] = columns_at(incident, which, incident.shape[2] // block, block)
    for shift in range(sections):
        parts[shift][...] = columns_at(phase, lax.rem(depth + shift, sections), sections, block)


def pack_kernel(entrance, *refs, sections, wanted):
    parts, sends = refs[:sections], refs[sections:]
    planes, rows, block = parts[0].shape
    depth, row = lax.axis_index("depth"), lax.axis_index("lat")

    def fill(distance, up, down):
        at = 0
        for slab in range(sections):
            kind = halo_kind(planes, rows, sections, slab, distance)
            source = lax.rem(depth - slab + sections, sections)
            take = lambda p: pick(source, [r[p] for r in parts])
            if kind == "full":
                for p in range(planes):
                    value = take(p)
                    for ref in (up, down):
                        if ref is not None:
                            ref[at + p] = value
                at += planes
            elif kind == "triangle":
                for p in range(planes // 2):
                    n = 2 * p + 1
                    value, other = take(p), take(planes - 1 - p)
                    if up is not None:
                        up[at + p] = value
                        up[at + p, 0:n, :] = other[rows - n :]
                    if down is not None:
                        down[at + p] = value
                        down[at + p, rows - n :, :] = other[:n]
                at += planes // 2
        for c in range(2):
            for ref in (up, down):
                if ref is not None:
                    ref[at + c] = entrance[c]

    for distance in sorted({d for d, _ in wanted}):
        pair = [sends[wanted.index((distance, q))] if (distance, q) in wanted else None for q in (0, 1)]
        for q in (0, 1):
            pl.when(lax.rem(row // distance, 2) == q)(functools.partial(fill, distance, pair[q], pair[1 - q]))


def march_kernel(*refs, sections, cores, wanted, reach):
    turn_refs, entrance, refs = refs[:cores], refs[cores], refs[cores + 1 :]
    parts, halos, refs = refs[:sections], refs[sections : sections + len(wanted)], refs[sections + len(wanted) :]
    outs, (v0, v1, w, cs, ss) = refs[:-5], refs[-5:]
    planes, rows, block = parts[0].shape
    angles = v0.shape[0]
    total = planes * sections
    width = reach * rows
    depth, row, lat = lax.axis_index("depth"), lax.axis_index("lat"), lax.axis_size("lat")

    blank = jnp.zeros((rows, block), jnp.float32)

    def sides(distance, at):
        even, odd = (halos[wanted.index((distance, q))][at] if (distance, q) in wanted else None for q in (0, 1))
        if even is None and odd is None:
            return blank, blank
        if even is None or odd is None:
            value = odd if even is None else even
            return value, value
        first = lax.rem(row // distance, 2) == 0
        return jnp.where(first, odd, even), jnp.where(first, even, odd)

    for distance in range(reach, 0, -1):
        lower, upper = row >= distance, row + distance < lat
        scales = [jnp.where(inside, amplitude, 0.0) for inside in (lower, upper)]
        places = (width - distance * rows, width + distance * rows)
        at = 0
        for slab in range(sections):
            kind = halo_kind(planes, rows, sections, slab, distance)
            first = slab * planes
            for p in range({None: 0, "full": planes, "triangle": planes // 2}[kind]):
                n = rows - 1 - 2 * p
                for place, scale, value, skew in zip(places, scales, sides(distance, at + p), (n, -n)):
                    for ref, entry in zip((ss, cs), scaled_sincos(value, scale)):
                        ref[first + p, place : place + rows, :] = entry
                        if kind == "triangle":
                            ref[first + planes - 1 - p, place + skew : place + skew + rows, :] = entry
            at += {None: 0, "full": planes, "triangle": planes // 2}[kind]
        for c in range(4):
            values = sides(distance, at + c) if c < 2 else (blank, blank)
            for place, inside, value in zip(places, (lower, upper), values):
                for a in range(angles):
                    v0[a, c, place : place + rows, :] = jnp.where(inside, value, 0.0)
    for c in range(4):
        for a in range(angles):
            v0[a, c, width : width + rows, :] = entrance[c] if c < 2 else blank
    for slab in range(sections):
        source = lax.rem(depth - slab + sections, sections)
        for p in range(planes):
            value = pick(source, [r[p] for r in parts])
            for ref, entry in zip((ss, cs), scaled_sincos(value, amplitude)):
                ref[slab * planes + p, width : width + rows, :] = entry

    def euler(ref, a, at, sine, cosine, turn):
        here = slice(at, at + 8)
        tr, ti, br, bi = (ref[a, c, here, :] for c in range(4))
        tr_back, ti_back = (ref[a, c, at - 1 : at + 7, :] for c in (0, 1))
        br_next, bi_next = (ref[a, c, at + 1 : at + 9, :] for c in (2, 3))
        return (
            (stay * tr + tr_back) - (sine * br + cosine * bi),
            (stay * ti + ti_back) + (cosine * br - sine * bi),
            (stay * br + br_next) - (cosine * ti - sine * tr) - turn * bi,
            (stay * bi + bi_next) + (cosine * tr + sine * ti) + turn * br,
        )

    turns = [ref[a] for ref in turn_refs for a in range(ref.shape[0])]
    now, later = v0, v1
    for p in range(total):
        span = 2 * (total - p) - 1
        for at in range(width - span, width + rows + span, 8):
            sine, cosine = ss[p, at : at + 8, :], cs[p, at : at + 8, :]
            for a in range(angles):
                for c, value in enumerate(euler(now, a, at, sine, cosine, turns[a])):
                    w[a, c, at : at + 8, :] = value
        span = 2 * (total - p) - 2
        for at in range(width - span, width + rows + span, 8):
            sine, cosine = ss[p, at : at + 8, :], cs[p, at : at + 8, :]
            for a in range(angles):
                for c, value in enumerate(euler(w, a, at, sine, cosine, turns[a])):
                    later[a, c, at : at + 8, :] = carry * now[a, c, at : at + 8, :] + value
        now, later = later, now
        if (p + 1) % planes == 0:
            shrink = (nu**2 / 2.0) ** (p + 1)
            shift = lax.rem(p // planes - depth + sections, sections)

            def leave(s, now=now, shrink=shrink):
                for a in range(angles):
                    for c in range(4):
                        outs[s * angles + a][c] = shrink * now[a, c, width : width + rows, :]

            for s in range(sections):
                pl.when(shift == s)(functools.partial(leave, s))


VMEM = pl.BlockSpec(memory_space=pltpu.VMEM)
SMEM = pl.BlockSpec(memory_space=pltpu.SMEM)
GRANT = pltpu.CompilerParams(vmem_limit_bytes=24 * 2**20)


def kernel_call(kernel, name, shapes, in_specs, scratch=()):
    return pl.pallas_call(
        kernel,
        out_shape=[jax.ShapeDtypeStruct(s, jnp.float32) for s in shapes],
        in_specs=in_specs,
        out_specs=[VMEM] * len(shapes),
        scratch_shapes=[pltpu.VMEM(s, jnp.float32) for s in scratch],
        compiler_params=GRANT,
        name=name,
    )


def on_device(incident, phase, deviation):
    planes, rows, columns = phase.shape
    lat, sections, cores = (lax.axis_size(a) for a in ("lat", "depth", "rock"))
    depth, core = lax.axis_index("depth"), lax.axis_index("rock")
    angles = cores * deviation.shape[0]
    block = columns // sections
    reach = -(-2 * planes * sections // rows)

    def route(value, shift, turn):
        pairs = []
        for d in range(sections):
            for c in range(cores):
                pairs.append((d * cores + c, (d + shift) % sections * cores + (c + turn) % cores))
        return lax.ppermute(value, ("depth", "rock"), pairs)

    shapes = [(2, rows, block), (deviation.shape[0], 8, block)] + [(planes, rows, block)] * sections
    split = functools.partial(columns_kernel, sections=sections)
    entrance, turns, *parts = kernel_call(split, "columns", shapes, [SMEM, VMEM, VMEM])(deviation, phase, incident)
    parts = [parts[0]] + [route(parts[s], s, 0) for s in range(1, sections)]
    turns = [turns] + [route(turns, 0, turn) for turn in range(1, cores)]

    wanted, pairs, shapes = [], [], []
    for distance in range(1, reach + 1):
        kinds = [halo_kind(planes, rows, sections, slab, distance) for slab in range(sections)]
        depths = sum({None: 0, "full": planes, "triangle": planes // 2}[kind] for kind in kinds)
        for parity in (0, 1):
            swap = swaps(lat, sections, cores, distance, parity)
            if swap is not None:
                wanted.append((distance, parity))
                pairs.append(swap)
                shapes.append((depths + 2, rows, block))
    pack = functools.partial(pack_kernel, sections=sections, wanted=wanted)
    sends = kernel_call(pack, "pack", shapes, [VMEM] * (1 + sections))(entrance, *parts)
    halos = [lax.ppermute(s, ("lat", "depth", "rock"), swap) for s, swap in zip(sends, pairs)]

    window = rows * (2 * reach + 1) + 16
    march = functools.partial(march_kernel, sections=sections, cores=cores, wanted=wanted, reach=reach)
    exits = kernel_call(
        march,
        "march",
        [(4, rows, block)] * (sections * angles),
        [VMEM] * (cores + 1 + sections + len(halos)),
        [(angles, 4, window, block)] * 3 + [(sections * planes, window, block)] * 2,
    )(*turns, entrance, *parts, *halos)

    pieces = {}
    for shift in range(sections):
        for turn in range(cores):
            piece = exits[shift * angles + turn]
            pieces[shift, turn] = piece if shift == 0 and turn == 0 else route(piece, shift, turn)
    tiles = []
    for c in range(cores):
        for d in range(sections):
            by_turn = []
            for turn in range(cores):
                by_turn.append(pick(lax.rem(depth - d + sections, sections), [pieces[s, turn] for s in range(sections)]))
            tiles.append(pick(lax.rem(core - c + cores, cores), by_turn))
    return jnp.concatenate(tiles, axis=2)[None, :, None]


def solution(mesh):
    placed = (
        P(None, ("groups", "lat"), None),
        P("depth", ("groups", "lat"), "rock"),
        P(("groups", "rock")),
    )
    return jax.shard_map(
        on_device,
        mesh=mesh,
        in_specs=placed,
        out_specs=P("depth", None, "rock", ("groups", "lat"), None),
        check_vma=False,
    )
```

time: 25 us -> 24.6 us (0.984)
  starting transfers between devices: 13.7 us -> 10 us
  waiting for transfers between devices: 6.4 us -> 9.16 us
  Pallas kernels: 1.53 us -> 2.13 us
    ppermute x5, waiting for transfers between devices: 2.18 us -> 6.11 us  [route(): return lax.ppermute(value, ('depth', 'rock'), pairs)]
    ppermute x6 -> x3, starting transfers between devices: 8.28 us -> 4.76 us  [on_device(): lax.ppermute(s, ('lat', 'depth', 'rock'), swap)]
    ppermute x6 -> x3, waiting for transfers between devices: 4.22 us -> 3.06 us  [on_device(): lax.ppermute(s, ('lat', 'depth', 'rock'), swap)]
    pallas_call x3, Pallas kernels: 1.53 us -> 2.13 us  [the longest x1 2.07 us: on_device(): kernel_call(march, 'march', [(4, rows, block)] * (sections * angles), [VM...]
  transfers between devices with their start and end apart: 11 -> 8, of which waited for: 4 -> 5; matrix products, arithmetic and copies ran while one was open for 0% -> 0% of each run, Pallas kernels for 0% -> 0%
where the time goes in v3:
time: 24.6 us; the launch traced here: 24.4 us
  starting transfers between devices  10 us (41%)
  waiting for transfers between devices  9.16 us (37%)
  Pallas kernels  2.13 us (9%)
  local copies, waits for them, and re-layouts  1.74 us (7%)
  between operations  0.69 us (3%)
  other arithmetic  0.68 us (3%)
    ppermute x5, waiting for transfers between devices, route(): return lax.ppermute(value, ('depth', 'rock'), pairs)  6.11 us
    ppermute x5, starting transfers between devices, route(): return lax.ppermute(value, ('depth', 'rock'), pairs)  5.24 us
    ppermute x3, starting transfers between devices, on_device(): lax.ppermute(s, ('lat', 'depth', 'rock'), swap)  4.76 us
    ppermute x3, waiting for transfers between devices, on_device(): lax.ppermute(s, ('lat', 'depth', 'rock'), swap)  3.06 us
    pallas_call x1, Pallas kernels, on_device(): kernel_call(march, 'march', [(4, rows, block)] * (sections * angles), [VM...  2.07 us
    unnamed x4, local copies, waits for them, and re-layouts  1.74 us
    broadcast_in_dim x1, other arithmetic, on_device(): return jnp.concatenate(tiles, axis=2)[None, :, None]  0.67 us
  transfers between devices with their start and end apart: 8, of which 5 were waited for; matrix products, arithmetic and copies ran while one was open for 0% of the time, Pallas kernels for 0%

profile of v3, /device:TPU:0, one launch (start us, length us, event | category | flops | bytes accessed | tf_op | source)
XLA Modules:
  0.0 24.4 jit_solution(130576566360346679)
XLA Ops:
  0.7 0.0 copy-start
  0.7 0.9 %copy-done = f32[8,16,256]{2,1,0:T(8,128)S(1)} copy-done((f32[8,16,256]{2,1,0:T(8,128)S(1)}, f32[8,16,256]{2,1,0:T(8,128)}, u32[]{:S(2)}) %copy-start) | copy-done | bytes 131096
  1.6 0.0 copy-start.1
  1.6 0.8 %copy-done.1 = f32[2,16,512]{2,1,0:T(8,128)S(1)} copy-done((f32[2,16,512]{2,1,0:T(8,128)S(1)}, f32[2,16,512]{2,1,0:T(8,128)}, u32[]{:S(2)}) %copy-start.1) | copy-done | bytes 65560
  2.4 3.0 %collective-permute-start.1 = (f32[8,16,128]{2,1,0:T(8,128)S(1)}, f32[8,16,128]{2,1,0:T(8,128)S(1)}, u32[]{:S(2)}, u32[]{:S(2)}) collective-permute-start(f32[8,16,128]{2,1,0:T(8,128)S(1)} %get-tuple-element.19), channel_id=1, source_target_pairs={{0,2},{1,3},{2,0},{3,1},{4,6},{5,7},{6,4},{7,5},{8,10},{9,11},{10,... | collective-permute-start | bytes 196616 | tf_op jit(solution)/shard_map/ppermute | solution.py:260
  5.4 2.2 %collective-permute-done.1.refs_1_.refs_4_ = f32[8,16,128]{2,1,0:T(8,128)S(1)} collective-permute-done((f32[8,16,128]{2,1,0:T(8,128)S(1)}, f32[8,16,128]{2,1,0:T(8,128)S(1)}, u32[]{:S(2)}, u32[]{:S(2)}) %collective-permute-start.1) | collective-permute-done | bytes 65568 | tf_op jit(solution)/shard_map/ppermute | solution.py:260
  7.7 2.2 %collective-permute-start.2 = (f32[14,16,128]{2,1,0:T(8,128)S(1)}, f32[14,16,128]{2,1,0:T(8,128)S(1)}, u32[]{:S(2)}, u32[]{:S(2)}) collective-permute-start(f32[14,16,128]{2,1,0:T(8,128)S(1)} %get-tuple-element.20), channel_id=1, source_target_pairs={{0,4},{1,5},{2,6},{3,7},{4,0},{5,1},{6,2},{7,3},{8,12},{9,13},{10,... | collective-permute-start | bytes 344072 | tf_op jit(solution)/shard_map/ppermute | solution.py:280
  9.9 0.0 collective-permute-start.3
  9.9 2.6 %collective-permute-start.4 = (f32[6,16,128]{2,1,0:T(8,128)S(1)}, f32[6,16,128]{2,1,0:T(8,128)S(1)}, u32[]{:S(2)}, u32[]{:S(2)}) collective-permute-start(f32[6,16,128]{2,1,0:T(8,128)S(1)} %get-tuple-element.22), channel_id=1, source_target_pairs={{0,8},{1,9},{2,10},{3,11},{4,12},{5,13},{6,14},{7,15},{8,0},{9,1},... | collective-permute-start | bytes 147464 | tf_op jit(solution)/shard_map/ppermute | solution.py:280
  12.5 0.0 collective-permute-start
  12.5 1.2 %collective-permute-done.refs_1_ = f32[1,8,128]{2,1,0:T(8,128)S(1)} collective-permute-done((f32[1,8,128]{2,1,0:T(8,128)S(1)}, f32[1,8,128]{2,1,0:T(8,128)S(1)}, u32[]{:S(2)}, u32[]{:S(2)}) %collective-permute-start) | collective-permute-done | bytes 4128 | tf_op jit(solution)/shard_map/ppermute | solution.py:260
  13.7 3.1 %collective-permute-done.4.refs_7_ = f32[6,16,128]{2,1,0:T(8,128)S(1)} collective-permute-done((f32[6,16,128]{2,1,0:T(8,128)S(1)}, f32[6,16,128]{2,1,0:T(8,128)S(1)}, u32[]{:S(2)}, u32[]{:S(2)}) %collective-permute-start.4) | collective-permute-done | bytes 49184 | tf_op jit(solution)/shard_map/ppermute | solution.py:280
  16.7 0.0 collective-permute-done.2.refs_5_
  16.7 0.0 collective-permute-done.3.refs_6_
  16.7 2.1 %march.1 = (f32[4,16,128]{2,1,0:T(8,128)S(1)}, f32[4,16,128]{2,1,0:T(8,128)S(1)}, f32[4,16,128]{2,1,0:T(8,128)S(1)}, f32[4,16,128]{2,1,0:T(8,128)S(1)}) custom-call(f32[1,8,128]{2,1,0:T(8,128)S(1)} %get-tuple-element.16.refs_0_, f32[1,8,128]{2,1,0:T(8,128)S(1)} %collective-permute-done.refs_1_, f32[2,16,128]{2,1,0:T(8,128)S(1)} %get-tuple-element.17.entrance.refs_2_, ...), custom_call_target="tpu_custom_call" | custom-call | tf_op jit(solution)/shard_map/march/pallas_call | solution.py:284
  18.8 1.6 %collective-permute-start.5 = (f32[4,16,128]{2,1,0:T(8,128)S(1)}, f32[4,16,128]{2,1,0:T(8,128)S(1)}, u32[]{:S(2)}, u32[]{:S(2)}) collective-permute-start(f32[4,16,128]{2,1,0:T(8,128)S(1)} %get-tuple-element.24), channel_id=1, source_target_pairs={{0,2},{1,3},{2,0},{3,1},{4,6},{5,7},{6,4},{7,5},{8,10},{9,11},{10,... | collective-permute-start | bytes 98312 | tf_op jit(solution)/shard_map/ppermute | solution.py:260
  20.4 0.0 collective-permute-start.6
  20.4 0.6 %collective-permute-start.7 = (f32[4,16,128]{2,1,0:T(8,128)S(1)}, f32[4,16,128]{2,1,0:T(8,128)S(1)}, u32[]{:S(2)}, u32[]{:S(2)}) collective-permute-start(f32[4,16,128]{2,1,0:T(8,128)S(1)} %get-tuple-element.26), channel_id=1, source_target_pairs={{0,3},{1,2},{2,1},{3,0},{4,7},{5,6},{6,5},{7,4},{8,11},{9,10},{10,... | collective-permute-start | bytes 98312 | tf_op jit(solution)/shard_map/ppermute | solution.py:260
  21.0 1.8 %collective-permute-done.5 = f32[4,16,128]{2,1,0:T(8,128)S(1)} collective-permute-done((f32[4,16,128]{2,1,0:T(8,128)S(1)}, f32[4,16,128]{2,1,0:T(8,128)S(1)}, u32[]{:S(2)}, u32[]{:S(2)}) %collective-permute-start.5) | collective-permute-done | bytes 32800 | tf_op jit(solution)/shard_map/ppermute | solution.py:260
  22.8 0.0 collective-permute-done.6
  22.8 0.9 %collective-permute-done.7 = f32[4,16,128]{2,1,0:T(8,128)S(1)} collective-permute-done((f32[4,16,128]{2,1,0:T(8,128)S(1)}, f32[4,16,128]{2,1,0:T(8,128)S(1)}, u32[]{:S(2)}, u32[]{:S(2)}) %collective-permute-start.7) | collective-permute-done | bytes 32800 | tf_op jit(solution)/shard_map/ppermute | solution.py:260
  23.7 0.7 %maximum_bitcast_fusion = f32[1,4,1,16,512]{4,3,2,1,0:T(8,128)} fusion(f32[4,16,128]{2,1,0:T(8,128)S(1)} %get-tuple-element.28, f32[4,16,128]{2,1,0:T(8,128)S(1)} %get-tuple-element.29, f32[4,16,128]{2,1,0:T(8,128)S(1)} %get-tuple-element.30, f32[4,16,128]{2,1,0:T(8,128)S(1)} %get-tuple-element.27), kind=kLoop, calls=%fused_computation | loop fusion | flops 98304 | bytes 262144 | tf_op jit(solution)/shard_map/broadcast_in_dim | solution.py:304
  (3 shorter events, 0.1 us)
Async XLA Ops:
  0.7 0.9 %copy-start = (f32[8,16,256]{2,1,0:T(8,128)S(1)}, f32[8,16,256]{2,1,0:T(8,128)}, u32[]{:S(2)}) copy-start(f32[8,16,256]{2,1,0:T(8,128)} %phase.1) | copy-start | bytes 393220
  1.6 0.8 %copy-start.1 = (f32[2,16,512]{2,1,0:T(8,128)S(1)}, f32[2,16,512]{2,1,0:T(8,128)}, u32[]{:S(2)}) copy-start(f32[2,16,512]{2,1,0:T(8,128)} %incident.1) | copy-start | bytes 196612
  2.4 5.3 %collective-permute-start.1 = (f32[8,16,128]{2,1,0:T(8,128)S(1)}, f32[8,16,128]{2,1,0:T(8,128)S(1)}, u32[]{:S(2)}, u32[]{:S(2)}) collective-permute-start(f32[8,16,128]{2,1,0:T(8,128)S(1)} %get-tuple-element.19), channel_id=1, source_target_pairs={{0,2},{1,3},{2,0},{3,1},{4,6},{5,7},{6,4},{7,5},{8,10},{9,11},{10,... | collective-permute-start | bytes 196616 | tf_op jit(solution)/shard_map/ppermute | solution.py:260
  7.7 9.0 %collective-permute-start.2 = (f32[14,16,128]{2,1,0:T(8,128)S(1)}, f32[14,16,128]{2,1,0:T(8,128)S(1)}, u32[]{:S(2)}, u32[]{:S(2)}) collective-permute-start(f32[14,16,128]{2,1,0:T(8,128)S(1)} %get-tuple-element.20), channel_id=1, source_target_pairs={{0,4},{1,5},{2,6},{3,7},{4,0},{5,1},{6,2},{7,3},{8,12},{9,13},{10,... | collective-permute-start | bytes 344072 | tf_op jit(solution)/shard_map/ppermute | solution.py:280
  9.9 6.8 %collective-permute-start.3 = (f32[14,16,128]{2,1,0:T(8,128)S(1)}, f32[14,16,128]{2,1,0:T(8,128)S(1)}, u32[]{:S(2)}, u32[]{:S(2)}) collective-permute-start(f32[14,16,128]{2,1,0:T(8,128)S(1)} %get-tuple-element.21), channel_id=1, source_target_pairs={{0,1},{1,0},{2,3},{3,2},{4,8},{5,9},{6,10},{7,11},{8,4},{9,5},{10,... | collective-permute-start | bytes 344072 | tf_op jit(solution)/shard_map/ppermute | solution.py:280
  9.9 6.8 %collective-permute-start.4 = (f32[6,16,128]{2,1,0:T(8,128)S(1)}, f32[6,16,128]{2,1,0:T(8,128)S(1)}, u32[]{:S(2)}, u32[]{:S(2)}) collective-permute-start(f32[6,16,128]{2,1,0:T(8,128)S(1)} %get-tuple-element.22), channel_id=1, source_target_pairs={{0,8},{1,9},{2,10},{3,11},{4,12},{5,13},{6,14},{7,15},{8,0},{9,1},... | collective-permute-start | bytes 147464 | tf_op jit(solution)/shard_map/ppermute | solution.py:280
  12.5 1.2 %collective-permute-start = (f32[1,8,128]{2,1,0:T(8,128)S(1)}, f32[1,8,128]{2,1,0:T(8,128)S(1)}, u32[]{:S(2)}, u32[]{:S(2)}) collective-permute-start(f32[1,8,128]{2,1,0:T(8,128)S(1)} %get-tuple-element.16.refs_0_), channel_id=1, source_target_pairs={{0,1},{1,0},{2,3},{3,2},{4,5},{5,4},{6,7},{7,6},{8,9},{9,8},{10,11... | collective-permute-start | bytes 12296 | tf_op jit(solution)/shard_map/ppermute | solution.py:260
  18.8 4.0 %collective-permute-start.5 = (f32[4,16,128]{2,1,0:T(8,128)S(1)}, f32[4,16,128]{2,1,0:T(8,128)S(1)}, u32[]{:S(2)}, u32[]{:S(2)}) collective-permute-start(f32[4,16,128]{2,1,0:T(8,128)S(1)} %get-tuple-element.24), channel_id=1, source_target_pairs={{0,2},{1,3},{2,0},{3,1},{4,6},{5,7},{6,4},{7,5},{8,10},{9,11},{10,... | collective-permute-start | bytes 98312 | tf_op jit(solution)/shard_map/ppermute | solution.py:260
  20.4 2.4 %collective-permute-start.6 = (f32[4,16,128]{2,1,0:T(8,128)S(1)}, f32[4,16,128]{2,1,0:T(8,128)S(1)}, u32[]{:S(2)}, u32[]{:S(2)}) collective-permute-start(f32[4,16,128]{2,1,0:T(8,128)S(1)} %get-tuple-element.25), channel_id=1, source_target_pairs={{0,1},{1,0},{2,3},{3,2},{4,5},{5,4},{6,7},{7,6},{8,9},{9,8},{10,11... | collective-permute-start | bytes 98312 | tf_op jit(solution)/shard_map/ppermute | solution.py:260
  20.4 3.3 %collective-permute-start.7 = (f32[4,16,128]{2,1,0:T(8,128)S(1)}, f32[4,16,128]{2,1,0:T(8,128)S(1)}, u32[]{:S(2)}, u32[]{:S(2)}) collective-permute-start(f32[4,16,128]{2,1,0:T(8,128)S(1)} %get-tuple-element.26), channel_id=1, source_target_pairs={{0,3},{1,2},{2,1},{3,0},{4,7},{5,6},{6,5},{7,4},{8,11},{9,10},{10,... | collective-permute-start | bytes 98312 | tf_op jit(solution)/shard_map/ppermute | solution.py:260

commit v4 on v3

--- a/solution.py
+++ b/solution.py
@@ -9,6 +9,7 @@
 from jax.experimental.pallas import tpu as pltpu
 from jax.sharding import PartitionSpec as P
 
+
 courant = np.float32(0.9)
 coupling = np.float32(0.2)
 
@@ -65,77 +66,110 @@
     return "triangle" if planes % 2 == 0 and need[0] == rows - 1 and rows == 2 * planes else "full"
 
 
-def swaps(lat, sections, cores, distance, parity):
+def swaps(lat, sections, cores, distance, parity, shift, useful):
     pairs, real = [], False
     for row in range(lat):
         other = row + distance if row // distance % 2 == parity else row - distance
         real |= 0 <= other < lat
         for depth in range(sections):
             for core in range(cores):
-                here = (row * sections + depth) * cores + core
-                if 0 <= other < lat:
-                    there = (other * sections + depth) * cores + core
-                else:
-                    there = (row * sections + depth) * cores + (core + 1) % cores
-                pairs.append((here, there))
+                target, aim, to = row, (depth + shift) % sections, core
+                if 0 <= other < lat and depth in useful:
+                    target = other
+                elif shift == 0 or not 0 <= other < lat:
+                    aim, to = depth, (core + 1) % cores
+                pairs.append(((row * sections + depth) * cores + core, (target * sections + aim) * cores + to))
+    assert len({b for _, b in pairs}) == len(pairs)
     return pairs if real else None
 
 
-def columns_kernel(detuning, phase, incident, *outs, sections):
-    block = outs[0].shape[2]
-    entrance, turns, parts = outs[0], outs[1], outs[2:]
-    depth = lax.axis_index("depth")
+def pieces_of(kind, planes):
+    return {None: 0, "full": planes, "triangle": planes // 2}[kind]
+
+
+def write_halo(kind, planes, rows, take, up, down, at):
+    for p in range(pieces_of(kind, planes)):
+        value = take(p)
+        for ref in (up, down):
+            if ref is not None:
+                ref[at + p] = value
+        if kind == "triangle":
+            n, other = 2 * p + 1, take(planes - 1 - p)
+            if up is not None:
+                up[at + p, 0:n, :] = other[rows - n :]
+            if down is not None:
+                down[at + p, rows - n :, :] = other[:n]
+
+
+def columns_kernel(detuning, phase_hbm, incident_hbm, *refs, sections, far):
+    outs, (phase, incident, sems) = refs[:-3], refs[-3:]
+    planes, rows, columns = phase.shape
+    block = columns // sections
+    entrance, turns, parts, sends = outs[0], outs[1], outs[2 : 2 + sections], outs[2 + sections :]
+    depth, row = lax.axis_index("depth"), lax.axis_index("lat")
+    mine = pl.ds(pl.multiple_of(lax.axis_index("rock") * columns, columns), columns)
+    loads = [
+        pltpu.make_async_copy(phase_hbm, phase, sems.at[0]),
+        pltpu.make_async_copy(incident_hbm.at[:, :, mine], incident, sems.at[1]),
+    ]
+    for load in loads:
+        load.start()
     for a in range(turns.shape[0]):
         turns[a] = jnp.full(turns.shape[1:], detuning[a] * (1.0 / nu))
-    which = lax.axis_index("rock") * sections + depth
-    entrance[...] = columns_at(incident, which, incident.shape[2] // block, block)
+    for load in loads:
+        load.wait()
+    entrance[...] = columns_at(incident, depth, sections, block)
     for shift in range(sections):
         parts[shift][...] = columns_at(phase, lax.rem(depth + shift, sections), sections, block)
 
-
-def pack_kernel(entrance, *refs, sections, wanted):
+    def fill(shift, kind, up, down):
+        at = up.shape[0] - 2 if up is not None else down.shape[0] - 2
+        write_halo(kind, planes, rows, lambda p: parts[shift][p], up, down, 0)
+        fields = columns_at(incident, lax.rem(depth + shift, sections), sections, block)
+        for ref in (up, down):
+            if ref is not None:
+                ref[at : at + 2] = fields
+
+    for distance, shift in sorted({(d, s) for d, _, s in far}):
+        pair = [sends[far.index((distance, q, shift))] if (distance, q, shift) in far else None for q in (0, 1)]
+        for slab in range(sections):
+            kind = halo_kind(planes, rows, sections, slab, distance)
+            if kind is None and slab > 0:
+                continue
+            for q in (0, 1):
+                here = (depth == slab) & (lax.rem(row // distance, 2) == q)
+                pl.when(here)(functools.partial(fill, shift, kind, pair[q], pair[1 - q]))
+
+
+def hand_on(source, target):
+    target[...] = source[...]
+
+
+def pack_kernel(entrance, *refs, sections):
     parts, sends = refs[:sections], refs[sections:]
-    planes, rows, block = parts[0].shape
+    planes, rows, _ = parts[0].shape
     depth, row = lax.axis_index("depth"), lax.axis_index("lat")
 
-    def fill(distance, up, down):
+    def fill(up, down):
         at = 0
         for slab in range(sections):
-            kind = halo_kind(planes, rows, sections, slab, distance)
+            kind = halo_kind(planes, rows, sections, slab, 1)
             source = lax.rem(depth - slab + sections, sections)
-            take = lambda p: pick(source, [r[p] for r in parts])
-            if kind == "full":
-                for p in range(planes):
-                    value = take(p)
-                    for ref in (up, down):
-                        if ref is not None:
-                            ref[at + p] = value
-                at += planes
-            elif kind == "triangle":
-                for p in range(planes // 2):
-                    n = 2 * p + 1
-                    value, other = take(p), take(planes - 1 - p)
-                    if up is not None:
-                        up[at + p] = value
-                        up[at + p, 0:n, :] = other[rows - n :]
-                    if down is not None:
-                        down[at + p] = value
-                        down[at + p, rows - n :, :] = other[:n]
-                at += planes // 2
-        for c in range(2):
-            for ref in (up, down):
-                if ref is not None:
-                    ref[at + c] = entrance[c]
-
-    for distance in sorted({d for d, _ in wanted}):
-        pair = [sends[wanted.index((distance, q))] if (distance, q) in wanted else None for q in (0, 1)]
-        for q in (0, 1):
-            pl.when(lax.rem(row // distance, 2) == q)(functools.partial(fill, distance, pair[q], pair[1 - q]))
-
-
-def march_kernel(*refs, sections, cores, wanted, reach):
+            write_halo(kind, planes, rows, lambda p: pick(source, [r[p] for r in parts]), up, down, at)
+            at += pieces_of(kind, planes)
+        for ref in (up, down):
+            if ref is not None:
+                ref[at : at + 2] = entrance[...]
+
+    pair = [sends[q] if q < len(sends) else None for q in (0, 1)]
+    for q in (0, 1):
+        pl.when(lax.rem(row, 2) == q)(functools.partial(fill, pair[q], pair[1 - q]))
+
+
+def march_kernel(*refs, sections, cores, near, far, reach):
     turn_refs, entrance, refs = refs[:cores], refs[cores], refs[cores + 1 :]
-    parts, halos, refs = refs[:sections], refs[sections : sections + len(wanted)], refs[sections + len(wanted) :]
+    parts, refs = refs[:sections], refs[sections:]
+    halos, refs = dict(zip(near + far, refs)), refs[len(near + far) :]
     outs, (v0, v1, w, cs, ss) = refs[:-5], refs[-5:]
     planes, rows, block = parts[0].shape
     angles = v0.shape[0]
@@ -145,13 +179,13 @@
 
     blank = jnp.zeros((rows, block), jnp.float32)
 
-    def sides(distance, at):
-        even, odd = (halos[wanted.index((distance, q))][at] if (distance, q) in wanted else None for q in (0, 1))
-        if even is None and odd is None:
-            return blank, blank
-        if even is None or odd is None:
-            value = odd if even is None else even
-            return value, value
+    def sides(distance, source, at):
+        even, odd = (
+            pick(source, [halos[distance, q, s][at] for s in range(sections if distance > 1 else 1)])
+            if (distance, q, 0) in halos
+            else blank
+            for q in (0, 1)
+        )
         first = lax.rem(row // distance, 2) == 0
         return jnp.where(first, odd, even), jnp.where(first, even, odd)
 
@@ -163,16 +197,20 @@
         for slab in range(sections):
             kind = halo_kind(planes, rows, sections, slab, distance)
             first = slab * planes
-            for p in range({None: 0, "full": planes, "triangle": planes // 2}[kind]):
+            source = lax.rem(depth - slab + sections, sections)
+            at = at if distance == 1 else 0
+            for p in range(pieces_of(kind, planes)):
                 n = rows - 1 - 2 * p
-                for place, scale, value, skew in zip(places, scales, sides(distance, at + p), (n, -n)):
+                for place, scale, value, skew in zip(places, scales, sides(distance, source, at + p), (n, -n)):
                     for ref, entry in zip((ss, cs), scaled_sincos(value, scale)):
                         ref[first + p, place : place + rows, :] = entry
                         if kind == "triangle":
                             ref[first + planes - 1 - p, place + skew : place + skew + rows, :] = entry
-            at += {None: 0, "full": planes, "triangle": planes // 2}[kind]
+            at += pieces_of(kind, planes)
+        if distance > 1:
+            at = max(pieces_of(halo_kind(planes, rows, sections, slab, distance), planes) for slab in range(sections))
         for c in range(4):
-            values = sides(distance, at + c) if c < 2 else (blank, blank)
+            values = sides(distance, depth, at + c) if c < 2 else (blank, blank)
             for place, inside, value in zip(places, (lower, upper), values):
                 for a in range(angles):
                     v0[a, c, place : place + rows, :] = jnp.where(inside, value, 0.0)
@@ -229,22 +267,22 @@
 
 VMEM = pl.BlockSpec(memory_space=pltpu.VMEM)
 SMEM = pl.BlockSpec(memory_space=pltpu.SMEM)
+HBM = pl.BlockSpec(memory_space=pltpu.HBM)
 GRANT = pltpu.CompilerParams(vmem_limit_bytes=24 * 2**20)
 
 
-def kernel_call(kernel, name, shapes, in_specs, scratch=()):
+def kernel_call(kernel, shapes, in_specs, scratch=()):
     return pl.pallas_call(
         kernel,
         out_shape=[jax.ShapeDtypeStruct(s, jnp.float32) for s in shapes],
         in_specs=in_specs,
         out_specs=[VMEM] * len(shapes),
-        scratch_shapes=[pltpu.VMEM(s, jnp.float32) for s in scratch],
+        scratch_shapes=[pltpu.VMEM(s, jnp.float32) if isinstance(s, tuple) else s for s in scratch],
         compiler_params=GRANT,
-        name=name,
     )
 
 
-def on_device(incident, phase, deviation):
+def scattered(incident, phase, deviation):
     planes, rows, columns = phase.shape
     lat, sections, cores = (lax.axis_size(a) for a in ("lat", "depth", "rock"))
     depth, core = lax.axis_index("depth"), lax.axis_index("rock")
@@ -259,31 +297,38 @@
                 pairs.append((d * cores + c, (d + shift) % sections * cores + (c + turn) % cores))
         return lax.ppermute(value, ("depth", "rock"), pairs)
 
-    shapes = [(2, rows, block), (deviation.shape[0], 8, block)] + [(planes, rows, block)] * sections
-    split = functools.partial(columns_kernel, sections=sections)
-    entrance, turns, *parts = kernel_call(split, "columns", shapes, [SMEM, VMEM, VMEM])(deviation, phase, incident)
+    near, far, routes, shapes = [], [], {}, []
+    for distance in range(1, reach + 1):
+        kinds = [halo_kind(planes, rows, sections, slab, distance) for slab in range(sections)]
+        useful = [slab for slab in range(sections) if slab == 0 or distance == 1 or kinds[slab]]
+        for shift in range(sections if distance > 1 else 1):
+            for parity in (0, 1):
+                swap = swaps(lat, sections, cores, distance, parity, shift, useful)
+                if swap is not None:
+                    (far if distance > 1 else near).append((distance, parity, shift))
+                    routes[distance, parity, shift] = swap
+                    if distance > 1:
+                        shapes.append((max(pieces_of(kind, planes) for kind in kinds) + 2, rows, block))
+    shapes = [(2, rows, block), (deviation.shape[0], 8, block)] + [(planes, rows, block)] * sections + shapes
+    split = functools.partial(columns_kernel, sections=sections, far=far)
+    scratch = [(planes, rows, columns), (2, rows, columns), pltpu.SemaphoreType.DMA((2,))]
+    stored = (pltpu.with_memory_space_constraint(a, pltpu.HBM) for a in (phase, incident))
+    entrance, turns, *parts = kernel_call(split, shapes, [SMEM, HBM, HBM], scratch)(deviation, *stored)
+    parts, sends = parts[:sections], parts[sections:]
+    everyone = ("lat", "depth", "rock")
     parts = [parts[0]] + [route(parts[s], s, 0) for s in range(1, sections)]
     turns = [turns] + [route(turns, 0, turn) for turn in range(1, cores)]
-
-    wanted, pairs, shapes = [], [], []
-    for distance in range(1, reach + 1):
-        kinds = [halo_kind(planes, rows, sections, slab, distance) for slab in range(sections)]
-        depths = sum({None: 0, "full": planes, "triangle": planes // 2}[kind] for kind in kinds)
-        for parity in (0, 1):
-            swap = swaps(lat, sections, cores, distance, parity)
-            if swap is not None:
-                wanted.append((distance, parity))
-                pairs.append(swap)
-                shapes.append((depths + 2, rows, block))
-    pack = functools.partial(pack_kernel, sections=sections, wanted=wanted)
-    sends = kernel_call(pack, "pack", shapes, [VMEM] * (1 + sections))(entrance, *parts)
-    halos = [lax.ppermute(s, ("lat", "depth", "rock"), swap) for s, swap in zip(sends, pairs)]
+    far_halos = [lax.ppermute(s, everyone, routes[key]) for s, key in zip(sends, far)]
+    (entrance,) = kernel_call(hand_on, [(2, rows, block)], [VMEM])(entrance)
+    depths = sum(pieces_of(halo_kind(planes, rows, sections, slab, 1), planes) for slab in range(sections))
+    pack = functools.partial(pack_kernel, sections=sections)
+    sends = kernel_call(pack, [(depths + 2, rows, block)] * len(near), [VMEM] * (1 + sections))(entrance, *parts)
+    halos = [lax.ppermute(s, everyone, routes[key]) for s, key in zip(sends, near)] + far_halos
 
     window = rows * (2 * reach + 1) + 16
-    march = functools.partial(march_kernel, sections=sections, cores=cores, wanted=wanted, reach=reach)
+    march = functools.partial(march_kernel, sections=sections, cores=cores, near=near, far=far, reach=reach)
     exits = kernel_call(
         march,
-        "march",
         [(4, rows, block)] * (sections * angles),
         [VMEM] * (cores + 1 + sections + len(halos)),
         [(angles, 4, window, block)] * 3 + [(sections * planes, window, block)] * 2,
@@ -311,7 +356,7 @@
         P(("groups", "rock")),
     )
     return jax.shard_map(
-        on_device,
+        scattered,
         mesh=mesh,
         in_specs=placed,
         out_specs=P("depth", None, "rock", ("groups", "lat"), None),

time: 24.6 us -> 26.4 us (1.073)
  local copies, waits for them, and re-layouts: 1.74 us -> 0 us
  waiting for transfers between devices: 9.16 us -> 10.6 us
  starting transfers between devices: 10 us -> 11.2 us
  Pallas kernels: 2.13 us -> 3.1 us
    unnamed x4 -> x0, local copies, waits for them, and re-layouts: 1.74 us -> none
    ppermute x3 -> x4, waiting for transfers between devices: 3.06 us -> 4.24 us  [scattered(): lax.ppermute(s, everyone, routes[key])]
    pallas_call x3 -> x4, Pallas kernels: 2.13 us -> 3.1 us  [the longest x1 2.12 us: scattered(): kernel_call(march, [(4, rows, block)] * (sections * angles), [VMEM] * (co...]
    ppermute x3 -> x4, starting transfers between devices: 4.76 us -> 5.69 us  [scattered(): lax.ppermute(s, everyone, routes[key])]
  transfers between devices with their start and end apart: 8 -> 9, of which waited for: 5 -> 5; matrix products, arithmetic and copies ran while one was open for 0% -> 0% of each run, Pallas kernels for 0% -> 0%
where the time goes in v4:
time: 26.4 us; the launch traced here: 26.2 us
  starting transfers between devices  11.2 us (42%)
  waiting for transfers between devices  10.6 us (40%)
  Pallas kernels  3.1 us (12%)
  between operations  0.69 us (3%)
  other arithmetic  0.68 us (3%)
    ppermute x5, waiting for transfers between devices, route(): return lax.ppermute(value, ('depth', 'rock'), pairs)  6.33 us
    ppermute x4, starting transfers between devices, scattered(): lax.ppermute(s, everyone, routes[key])  5.69 us
    ppermute x5, starting transfers between devices, route(): return lax.ppermute(value, ('depth', 'rock'), pairs)  5.5 us
    ppermute x4, waiting for transfers between devices, scattered(): lax.ppermute(s, everyone, routes[key])  4.24 us
    pallas_call x1, Pallas kernels, scattered(): kernel_call(march, [(4, rows, block)] * (sections * angles), [VMEM] * (co...  2.12 us
    pallas_call x1, Pallas kernels, scattered(): kernel_call(split, shapes, [SMEM, HBM, HBM], scratch)(deviation, *stored)  0.95 us
    broadcast_in_dim x1, other arithmetic, scattered(): return jnp.concatenate(tiles, axis=2)[None, :, None]  0.67 us
  transfers between devices with their start and end apart: 9, of which 5 were waited for; matrix products, arithmetic and copies ran while one was open for 0% of the time, Pallas kernels for 0%

profile of v4, /device:TPU:0, one launch (start us, length us, event | category | flops | bytes accessed | tf_op | source)
XLA Modules:
  0.0 26.2 jit_solution(14882737161055037585)
XLA Ops:
  0.7 1.0 %shard_map.37 = (f32[2,16,128]{2,1,0:T(8,128)S(1)}, f32[1,8,128]{2,1,0:T(8,128)S(1)}, f32[8,16,128]{2,1,0:T(8,128)S(1)}, f32[8,16,128]{2,1,0:T(8,128)S(1)}, f32[...) custom-call(f32[1]{0:T(128)S(6)} %copy.5.detuning, f32[8,16,256]{2,1,0:T(8,128)} %phase_hbm.1, f32[2,16,512]{2,1,0:T(8,128)} %incident_hbm.1), custom_call_target="tpu_custom_call" | custom-call | tf_op jit(solution)/shard_map/pallas_call | solution.py:316
  1.6 3.0 %collective-permute-start.1 = (f32[8,16,128]{2,1,0:T(8,128)S(1)}, f32[8,16,128]{2,1,0:T(8,128)S(1)}, u32[]{:S(2)}, u32[]{:S(2)}) collective-permute-start(f32[8,16,128]{2,1,0:T(8,128)S(1)} %get-tuple-element.20), channel_id=1, source_target_pairs={{0,2},{1,3},{2,0},{3,1},{4,6},{5,7},{6,4},{7,5},{8,10},{9,11},{10,... | collective-permute-start | bytes 196616 | tf_op jit(solution)/shard_map/ppermute | solution.py:298
  4.6 2.2 %collective-permute-done.1.refs_1_.refs_4_ = f32[8,16,128]{2,1,0:T(8,128)S(1)} collective-permute-done((f32[8,16,128]{2,1,0:T(8,128)S(1)}, f32[8,16,128]{2,1,0:T(8,128)S(1)}, u32[]{:S(2)}, u32[]{:S(2)}) %collective-permute-start.1) | collective-permute-done | bytes 65568 | tf_op jit(solution)/shard_map/ppermute | solution.py:298
  6.9 2.2 %collective-permute-start.2 = (f32[14,16,128]{2,1,0:T(8,128)S(1)}, f32[14,16,128]{2,1,0:T(8,128)S(1)}, u32[]{:S(2)}, u32[]{:S(2)}) collective-permute-start(f32[14,16,128]{2,1,0:T(8,128)S(1)} %get-tuple-element.21), channel_id=1, source_target_pairs={{0,4},{1,5},{2,6},{3,7},{4,0},{5,1},{6,2},{7,3},{8,12},{9,13},{10,... | collective-permute-start | bytes 344072 | tf_op jit(solution)/shard_map/ppermute | solution.py:326
  9.1 0.0 collective-permute-start.3
  9.1 2.6 %collective-permute-start.4 = (f32[6,16,128]{2,1,0:T(8,128)S(1)}, f32[6,16,128]{2,1,0:T(8,128)S(1)}, u32[]{:S(2)}, u32[]{:S(2)}) collective-permute-start(f32[6,16,128]{2,1,0:T(8,128)S(1)} %get-tuple-element.23), channel_id=1, source_target_pairs={{0,8},{1,9},{2,3},{3,2},{4,12},{5,13},{6,7},{7,6},{8,0},{9,1},{10,... | collective-permute-start | bytes 147464 | tf_op jit(solution)/shard_map/ppermute | solution.py:321
  11.7 0.9 %collective-permute-start.5 = (f32[6,16,128]{2,1,0:T(8,128)S(1)}, f32[6,16,128]{2,1,0:T(8,128)S(1)}, u32[]{:S(2)}, u32[]{:S(2)}) collective-permute-start(f32[6,16,128]{2,1,0:T(8,128)S(1)} %get-tuple-element.24), channel_id=1, source_target_pairs={{0,10},{1,11},{2,0},{3,1},{4,14},{5,15},{6,4},{7,5},{8,2},{9,3},{1... | collective-permute-start | bytes 147464 | tf_op jit(solution)/shard_map/ppermute | solution.py:321
  12.6 0.2 collective-permute-start
  12.8 0.9 %collective-permute-done.refs_1_ = f32[1,8,128]{2,1,0:T(8,128)S(1)} collective-permute-done((f32[1,8,128]{2,1,0:T(8,128)S(1)}, f32[1,8,128]{2,1,0:T(8,128)S(1)}, u32[]{:S(2)}, u32[]{:S(2)}) %collective-permute-start) | collective-permute-done | bytes 4128 | tf_op jit(solution)/shard_map/ppermute | solution.py:298
  13.8 4.2 %collective-permute-done.4.refs_7_ = f32[6,16,128]{2,1,0:T(8,128)S(1)} collective-permute-done((f32[6,16,128]{2,1,0:T(8,128)S(1)}, f32[6,16,128]{2,1,0:T(8,128)S(1)}, u32[]{:S(2)}, u32[]{:S(2)}) %collective-permute-start.4) | collective-permute-done | bytes 49184 | tf_op jit(solution)/shard_map/ppermute | solution.py:321
  18.0 0.0 collective-permute-done.5.refs_8_
  18.0 0.0 collective-permute-done.2.refs_5_
  18.0 0.0 collective-permute-done.3.refs_6_
  18.0 2.1 %shard_map.40 = (f32[4,16,128]{2,1,0:T(8,128)S(1)}, f32[4,16,128]{2,1,0:T(8,128)S(1)}, f32[4,16,128]{2,1,0:T(8,128)S(1)}, f32[4,16,128]{2,1,0:T(8,128)S(1)}) custom-call(f32[1,8,128]{2,1,0:T(8,128)S(1)} %get-tuple-element.17.refs_0_, f32[1,8,128]{2,1,0:T(8,128)S(1)} %collective-permute-done.refs_1_, f32[2,16,128]{2,1,0:T(8,128)S(1)} %shard_map.38.entrance.refs_2_, ...), custom_call_target="tpu_custom_call" | custom-call | tf_op jit(solution)/shard_map/pallas_call | solution.py:330
  20.1 2.0 %collective-permute-start.6 = (f32[4,16,128]{2,1,0:T(8,128)S(1)}, f32[4,16,128]{2,1,0:T(8,128)S(1)}, u32[]{:S(2)}, u32[]{:S(2)}) collective-permute-start(f32[4,16,128]{2,1,0:T(8,128)S(1)} %get-tuple-element.26), channel_id=1, source_target_pairs={{0,2},{1,3},{2,0},{3,1},{4,6},{5,7},{6,4},{7,5},{8,10},{9,11},{10,... | collective-permute-start | bytes 98312 | tf_op jit(solution)/shard_map/ppermute | solution.py:298
  22.2 0.0 collective-permute-start.7
  22.2 0.2 collective-permute-start.8
  22.4 1.7 %collective-permute-done.6 = f32[4,16,128]{2,1,0:T(8,128)S(1)} collective-permute-done((f32[4,16,128]{2,1,0:T(8,128)S(1)}, f32[4,16,128]{2,1,0:T(8,128)S(1)}, u32[]{:S(2)}, u32[]{:S(2)}) %collective-permute-start.6) | collective-permute-done | bytes 32800 | tf_op jit(solution)/shard_map/ppermute | solution.py:298
  24.1 0.0 collective-permute-done.7
  24.1 1.4 %collective-permute-done.8 = f32[4,16,128]{2,1,0:T(8,128)S(1)} collective-permute-done((f32[4,16,128]{2,1,0:T(8,128)S(1)}, f32[4,16,128]{2,1,0:T(8,128)S(1)}, u32[]{:S(2)}, u32[]{:S(2)}) %collective-permute-start.8) | collective-permute-done | bytes 32800 | tf_op jit(solution)/shard_map/ppermute | solution.py:298
  25.6 0.7 %maximum_bitcast_fusion = f32[1,4,1,16,512]{4,3,2,1,0:T(8,128)} fusion(f32[4,16,128]{2,1,0:T(8,128)S(1)} %get-tuple-element.30, f32[4,16,128]{2,1,0:T(8,128)S(1)} %get-tuple-element.31, f32[4,16,128]{2,1,0:T(8,128)S(1)} %get-tuple-element.32, f32[4,16,128]{2,1,0:T(8,128)S(1)} %get-tuple-element.29), kind=kLoop, calls=%fused_computation | loop fusion | flops 98304 | bytes 262144 | tf_op jit(solution)/shard_map/broadcast_in_dim | solution.py:349
  (3 shorter events, 0.0 us)
Async XLA Ops:
  1.6 5.3 %collective-permute-start.1 = (f32[8,16,128]{2,1,0:T(8,128)S(1)}, f32[8,16,128]{2,1,0:T(8,128)S(1)}, u32[]{:S(2)}, u32[]{:S(2)}) collective-permute-start(f32[8,16,128]{2,1,0:T(8,128)S(1)} %get-tuple-element.20), channel_id=1, source_target_pairs={{0,2},{1,3},{2,0},{3,1},{4,6},{5,7},{6,4},{7,5},{8,10},{9,11},{10,... | collective-permute-start | bytes 196616 | tf_op jit(solution)/shard_map/ppermute | solution.py:298
  6.9 11.1 %collective-permute-start.2 = (f32[14,16,128]{2,1,0:T(8,128)S(1)}, f32[14,16,128]{2,1,0:T(8,128)S(1)}, u32[]{:S(2)}, u32[]{:S(2)}) collective-permute-start(f32[14,16,128]{2,1,0:T(8,128)S(1)} %get-tuple-element.21), channel_id=1, source_target_pairs={{0,4},{1,5},{2,6},{3,7},{4,0},{5,1},{6,2},{7,3},{8,12},{9,13},{10,... | collective-permute-start | bytes 344072 | tf_op jit(solution)/shard_map/ppermute | solution.py:326
  9.1 8.9 %collective-permute-start.3 = (f32[14,16,128]{2,1,0:T(8,128)S(1)}, f32[14,16,128]{2,1,0:T(8,128)S(1)}, u32[]{:S(2)}, u32[]{:S(2)}) collective-permute-start(f32[14,16,128]{2,1,0:T(8,128)S(1)} %get-tuple-element.22), channel_id=1, source_target_pairs={{0,1},{1,0},{2,3},{3,2},{4,8},{5,9},{6,10},{7,11},{8,4},{9,5},{10,... | collective-permute-start | bytes 344072 | tf_op jit(solution)/shard_map/ppermute | solution.py:326
  9.1 8.9 %collective-permute-start.4 = (f32[6,16,128]{2,1,0:T(8,128)S(1)}, f32[6,16,128]{2,1,0:T(8,128)S(1)}, u32[]{:S(2)}, u32[]{:S(2)}) collective-permute-start(f32[6,16,128]{2,1,0:T(8,128)S(1)} %get-tuple-element.23), channel_id=1, source_target_pairs={{0,8},{1,9},{2,3},{3,2},{4,12},{5,13},{6,7},{7,6},{8,0},{9,1},{10,... | collective-permute-start | bytes 147464 | tf_op jit(solution)/shard_map/ppermute | solution.py:321
  11.7 6.3 %collective-permute-start.5 = (f32[6,16,128]{2,1,0:T(8,128)S(1)}, f32[6,16,128]{2,1,0:T(8,128)S(1)}, u32[]{:S(2)}, u32[]{:S(2)}) collective-permute-start(f32[6,16,128]{2,1,0:T(8,128)S(1)} %get-tuple-element.24), channel_id=1, source_target_pairs={{0,10},{1,11},{2,0},{3,1},{4,14},{5,15},{6,4},{7,5},{8,2},{9,3},{1... | collective-permute-start | bytes 147464 | tf_op jit(solution)/shard_map/ppermute | solution.py:321
  12.6 1.2 %collective-permute-start = (f32[1,8,128]{2,1,0:T(8,128)S(1)}, f32[1,8,128]{2,1,0:T(8,128)S(1)}, u32[]{:S(2)}, u32[]{:S(2)}) collective-permute-start(f32[1,8,128]{2,1,0:T(8,128)S(1)} %get-tuple-element.17.refs_0_), channel_id=1, source_target_pairs={{0,1},{1,0},{2,3},{3,2},{4,5},{5,4},{6,7},{7,6},{8,9},{9,8},{10,11... | collective-permute-start | bytes 12296 | tf_op jit(solution)/shard_map/ppermute | solution.py:298
  20.1 4.0 %collective-permute-start.6 = (f32[4,16,128]{2,1,0:T(8,128)S(1)}, f32[4,16,128]{2,1,0:T(8,128)S(1)}, u32[]{:S(2)}, u32[]{:S(2)}) collective-permute-start(f32[4,16,128]{2,1,0:T(8,128)S(1)} %get-tuple-element.26), channel_id=1, source_target_pairs={{0,2},{1,3},{2,0},{3,1},{4,6},{5,7},{6,4},{7,5},{8,10},{9,11},{10,... | collective-permute-start | bytes 98312 | tf_op jit(solution)/shard_map/ppermute | solution.py:298
  22.2 1.9 %collective-permute-start.7 = (f32[4,16,128]{2,1,0:T(8,128)S(1)}, f32[4,16,128]{2,1,0:T(8,128)S(1)}, u32[]{:S(2)}, u32[]{:S(2)}) collective-permute-start(f32[4,16,128]{2,1,0:T(8,128)S(1)} %get-tuple-element.27), channel_id=1, source_target_pairs={{0,1},{1,0},{2,3},{3,2},{4,5},{5,4},{6,7},{7,6},{8,9},{9,8},{10,11... | collective-permute-start | bytes 98312 | tf_op jit(solution)/shard_map/ppermute | solution.py:298
  22.2 3.3 %collective-permute-start.8 = (f32[4,16,128]{2,1,0:T(8,128)S(1)}, f32[4,16,128]{2,1,0:T(8,128)S(1)}, u32[]{:S(2)}, u32[]{:S(2)}) collective-permute-start(f32[4,16,128]{2,1,0:T(8,128)S(1)} %get-tuple-element.28), channel_id=1, source_target_pairs={{0,3},{1,2},{2,1},{3,0},{4,7},{5,6},{6,5},{7,4},{8,11},{9,10},{10,... | collective-permute-start | bytes 98312 | tf_op jit(solution)/shard_map/ppermute | solution.py:298

commit v5 on v4

--- a/solution.py
+++ b/solution.py
@@ -201,7 +201,9 @@
             at = at if distance == 1 else 0
             for p in range(pieces_of(kind, planes)):
                 n = rows - 1 - 2 * p
-                for place, scale, value, skew in zip(places, scales, sides(distance, source, at + p), (n, -n)):
+                blocks = sides(distance, source, at + p)
+                for place, inside, scale, value, skew in zip(places, (lower, upper), scales, blocks, (n, -n)):
+                    value = jnp.where(inside, value, 0.0)
                     for ref, entry in zip((ss, cs), scaled_sincos(value, scale)):
                         ref[first + p, place : place + rows, :] = entry
                         if kind == "triangle":
@@ -318,12 +320,17 @@
     everyone = ("lat", "depth", "rock")
     parts = [parts[0]] + [route(parts[s], s, 0) for s in range(1, sections)]
     turns = [turns] + [route(turns, 0, turn) for turn in range(1, cores)]
-    far_halos = [lax.ppermute(s, everyone, routes[key]) for s, key in zip(sends, far)]
+    far_halos = []
+    for key, send in zip(far, sends):
+        far_halos.append(lax.ppermute(send, everyone, routes[key]))
     (entrance,) = kernel_call(hand_on, [(2, rows, block)], [VMEM])(entrance)
     depths = sum(pieces_of(halo_kind(planes, rows, sections, slab, 1), planes) for slab in range(sections))
     pack = functools.partial(pack_kernel, sections=sections)
     sends = kernel_call(pack, [(depths + 2, rows, block)] * len(near), [VMEM] * (1 + sections))(entrance, *parts)
-    halos = [lax.ppermute(s, everyone, routes[key]) for s, key in zip(sends, near)] + far_halos
+    halos = []
+    for key, send in zip(near, sends):
+        halos.append(lax.ppermute(send, everyone, routes[key]))
+    halos += far_halos
 
     window = rows * (2 * reach + 1) + 16
     march = functools.partial(march_kernel, sections=sections, cores=cores, near=near, far=far, reach=reach)

time: 26.4 us -> 26.4 us (level)
  no operation moved by 1% of the time
where the time goes in v5:
time: 26.4 us; the launch traced here: 26.2 us
  starting transfers between devices  11.2 us (42%)
  waiting for transfers between devices  10.6 us (40%)
  Pallas kernels  3.1 us (12%)
  between operations  0.69 us (3%)
  other arithmetic  0.68 us (3%)
    ppermute x5, waiting for transfers between devices, route(): return lax.ppermute(value, ('depth', 'rock'), pairs)  6.33 us
    ppermute x5, starting transfers between devices, route(): return lax.ppermute(value, ('depth', 'rock'), pairs)  5.5 us
    ppermute x2, waiting for transfers between devices, scattered(): far_halos.append(lax.ppermute(send, everyone, routes[key]))  4.23 us
    ppermute x2, starting transfers between devices, scattered(): far_halos.append(lax.ppermute(send, everyone, routes[key]))  3.52 us
    ppermute x2, starting transfers between devices, scattered(): halos.append(lax.ppermute(send, everyone, routes[key]))  2.17 us
    pallas_call x1, Pallas kernels, scattered(): kernel_call(march, [(4, rows, block)] * (sections * angles), [VMEM] * (co...  2.12 us
    pallas_call x1, Pallas kernels, scattered(): kernel_call(split, shapes, [SMEM, HBM, HBM], scratch)(deviation, *stored)  0.95 us
    broadcast_in_dim x1, other arithmetic, scattered(): return jnp.concatenate(tiles, axis=2)[None, :, None]  0.67 us
  transfers between devices with their start and end apart: 9, of which 5 were waited for; matrix products, arithmetic and copies ran while one was open for 0% of the time, Pallas kernels for 0%

profile of v5, /device:TPU:0, one launch (start us, length us, event | category | flops | bytes accessed | tf_op | source)
XLA Modules:
  0.0 26.2 jit_solution(10439409397657335972)
XLA Ops:
  0.7 1.0 %shard_map.37 = (f32[2,16,128]{2,1,0:T(8,128)S(1)}, f32[1,8,128]{2,1,0:T(8,128)S(1)}, f32[8,16,128]{2,1,0:T(8,128)S(1)}, f32[8,16,128]{2,1,0:T(8,128)S(1)}, f32[...) custom-call(f32[1]{0:T(128)S(6)} %copy.5.detuning, f32[8,16,256]{2,1,0:T(8,128)} %phase_hbm.1, f32[2,16,512]{2,1,0:T(8,128)} %incident_hbm.1), custom_call_target="tpu_custom_call" | custom-call | tf_op jit(solution)/shard_map/pallas_call | solution.py:318
  1.6 3.0 %collective-permute-start.1 = (f32[8,16,128]{2,1,0:T(8,128)S(1)}, f32[8,16,128]{2,1,0:T(8,128)S(1)}, u32[]{:S(2)}, u32[]{:S(2)}) collective-permute-start(f32[8,16,128]{2,1,0:T(8,128)S(1)} %get-tuple-element.20), channel_id=1, source_target_pairs={{0,2},{1,3},{2,0},{3,1},{4,6},{5,7},{6,4},{7,5},{8,10},{9,11},{10,... | collective-permute-start | bytes 196616 | tf_op jit(solution)/shard_map/ppermute | solution.py:300
  4.6 2.2 %collective-permute-done.1.refs_1_.refs_4_ = f32[8,16,128]{2,1,0:T(8,128)S(1)} collective-permute-done((f32[8,16,128]{2,1,0:T(8,128)S(1)}, f32[8,16,128]{2,1,0:T(8,128)S(1)}, u32[]{:S(2)}, u32[]{:S(2)}) %collective-permute-start.1) | collective-permute-done | bytes 65568 | tf_op jit(solution)/shard_map/ppermute | solution.py:300
  6.9 2.2 %collective-permute-start.2 = (f32[14,16,128]{2,1,0:T(8,128)S(1)}, f32[14,16,128]{2,1,0:T(8,128)S(1)}, u32[]{:S(2)}, u32[]{:S(2)}) collective-permute-start(f32[14,16,128]{2,1,0:T(8,128)S(1)} %get-tuple-element.21), channel_id=1, source_target_pairs={{0,4},{1,5},{2,6},{3,7},{4,0},{5,1},{6,2},{7,3},{8,12},{9,13},{10,... | collective-permute-start | bytes 344072 | tf_op jit(solution)/shard_map/ppermute | solution.py:332
  9.1 0.0 collective-permute-start.3
  9.1 2.6 %collective-permute-start.4 = (f32[6,16,128]{2,1,0:T(8,128)S(1)}, f32[6,16,128]{2,1,0:T(8,128)S(1)}, u32[]{:S(2)}, u32[]{:S(2)}) collective-permute-start(f32[6,16,128]{2,1,0:T(8,128)S(1)} %get-tuple-element.23), channel_id=1, source_target_pairs={{0,8},{1,9},{2,3},{3,2},{4,12},{5,13},{6,7},{7,6},{8,0},{9,1},{10,... | collective-permute-start | bytes 147464 | tf_op jit(solution)/shard_map/ppermute | solution.py:325
  11.7 0.9 %collective-permute-start.5 = (f32[6,16,128]{2,1,0:T(8,128)S(1)}, f32[6,16,128]{2,1,0:T(8,128)S(1)}, u32[]{:S(2)}, u32[]{:S(2)}) collective-permute-start(f32[6,16,128]{2,1,0:T(8,128)S(1)} %get-tuple-element.24), channel_id=1, source_target_pairs={{0,10},{1,11},{2,0},{3,1},{4,14},{5,15},{6,4},{7,5},{8,2},{9,3},{1... | collective-permute-start | bytes 147464 | tf_op jit(solution)/shard_map/ppermute | solution.py:325
  12.6 0.2 collective-permute-start
  12.8 0.9 %collective-permute-done.refs_1_ = f32[1,8,128]{2,1,0:T(8,128)S(1)} collective-permute-done((f32[1,8,128]{2,1,0:T(8,128)S(1)}, f32[1,8,128]{2,1,0:T(8,128)S(1)}, u32[]{:S(2)}, u32[]{:S(2)}) %collective-permute-start) | collective-permute-done | bytes 4128 | tf_op jit(solution)/shard_map/ppermute | solution.py:300
  13.8 4.2 %collective-permute-done.4.refs_7_ = f32[6,16,128]{2,1,0:T(8,128)S(1)} collective-permute-done((f32[6,16,128]{2,1,0:T(8,128)S(1)}, f32[6,16,128]{2,1,0:T(8,128)S(1)}, u32[]{:S(2)}, u32[]{:S(2)}) %collective-permute-start.4) | collective-permute-done | bytes 49184 | tf_op jit(solution)/shard_map/ppermute | solution.py:325
  18.0 0.0 collective-permute-done.5.refs_8_
  18.0 0.0 collective-permute-done.2.refs_5_
  18.0 0.0 collective-permute-done.3.refs_6_
  18.0 2.1 %shard_map.40 = (f32[4,16,128]{2,1,0:T(8,128)S(1)}, f32[4,16,128]{2,1,0:T(8,128)S(1)}, f32[4,16,128]{2,1,0:T(8,128)S(1)}, f32[4,16,128]{2,1,0:T(8,128)S(1)}) custom-call(f32[1,8,128]{2,1,0:T(8,128)S(1)} %get-tuple-element.17.refs_0_, f32[1,8,128]{2,1,0:T(8,128)S(1)} %collective-permute-done.refs_1_, f32[2,16,128]{2,1,0:T(8,128)S(1)} %shard_map.38.entrance.refs_2_, ...), custom_call_target="tpu_custom_call" | custom-call | tf_op jit(solution)/shard_map/pallas_call | solution.py:337
  20.2 2.0 %collective-permute-start.6 = (f32[4,16,128]{2,1,0:T(8,128)S(1)}, f32[4,16,128]{2,1,0:T(8,128)S(1)}, u32[]{:S(2)}, u32[]{:S(2)}) collective-permute-start(f32[4,16,128]{2,1,0:T(8,128)S(1)} %get-tuple-element.26), channel_id=1, source_target_pairs={{0,2},{1,3},{2,0},{3,1},{4,6},{5,7},{6,4},{7,5},{8,10},{9,11},{10,... | collective-permute-start | bytes 98312 | tf_op jit(solution)/shard_map/ppermute | solution.py:300
  22.2 0.0 collective-permute-start.7
  22.2 0.2 collective-permute-start.8
  22.4 1.7 %collective-permute-done.6 = f32[4,16,128]{2,1,0:T(8,128)S(1)} collective-permute-done((f32[4,16,128]{2,1,0:T(8,128)S(1)}, f32[4,16,128]{2,1,0:T(8,128)S(1)}, u32[]{:S(2)}, u32[]{:S(2)}) %collective-permute-start.6) | collective-permute-done | bytes 32800 | tf_op jit(solution)/shard_map/ppermute | solution.py:300
  24.1 0.0 collective-permute-done.7
  24.1 1.4 %collective-permute-done.8 = f32[4,16,128]{2,1,0:T(8,128)S(1)} collective-permute-done((f32[4,16,128]{2,1,0:T(8,128)S(1)}, f32[4,16,128]{2,1,0:T(8,128)S(1)}, u32[]{:S(2)}, u32[]{:S(2)}) %collective-permute-start.8) | collective-permute-done | bytes 32800 | tf_op jit(solution)/shard_map/ppermute | solution.py:300
  25.6 0.7 %maximum_bitcast_fusion = f32[1,4,1,16,512]{4,3,2,1,0:T(8,128)} fusion(f32[4,16,128]{2,1,0:T(8,128)S(1)} %get-tuple-element.30, f32[4,16,128]{2,1,0:T(8,128)S(1)} %get-tuple-element.31, f32[4,16,128]{2,1,0:T(8,128)S(1)} %get-tuple-element.32, f32[4,16,128]{2,1,0:T(8,128)S(1)} %get-tuple-element.29), kind=kLoop, calls=%fused_computation | loop fusion | flops 98304 | bytes 262144 | tf_op jit(solution)/shard_map/broadcast_in_dim | solution.py:356
  (3 shorter events, 0.0 us)
Async XLA Ops:
  1.6 5.3 %collective-permute-start.1 = (f32[8,16,128]{2,1,0:T(8,128)S(1)}, f32[8,16,128]{2,1,0:T(8,128)S(1)}, u32[]{:S(2)}, u32[]{:S(2)}) collective-permute-start(f32[8,16,128]{2,1,0:T(8,128)S(1)} %get-tuple-element.20), channel_id=1, source_target_pairs={{0,2},{1,3},{2,0},{3,1},{4,6},{5,7},{6,4},{7,5},{8,10},{9,11},{10,... | collective-permute-start | bytes 196616 | tf_op jit(solution)/shard_map/ppermute | solution.py:300
  6.9 11.1 %collective-permute-start.2 = (f32[14,16,128]{2,1,0:T(8,128)S(1)}, f32[14,16,128]{2,1,0:T(8,128)S(1)}, u32[]{:S(2)}, u32[]{:S(2)}) collective-permute-start(f32[14,16,128]{2,1,0:T(8,128)S(1)} %get-tuple-element.21), channel_id=1, source_target_pairs={{0,4},{1,5},{2,6},{3,7},{4,0},{5,1},{6,2},{7,3},{8,12},{9,13},{10,... | collective-permute-start | bytes 344072 | tf_op jit(solution)/shard_map/ppermute | solution.py:332
  9.1 8.9 %collective-permute-start.3 = (f32[14,16,128]{2,1,0:T(8,128)S(1)}, f32[14,16,128]{2,1,0:T(8,128)S(1)}, u32[]{:S(2)}, u32[]{:S(2)}) collective-permute-start(f32[14,16,128]{2,1,0:T(8,128)S(1)} %get-tuple-element.22), channel_id=1, source_target_pairs={{0,1},{1,0},{2,3},{3,2},{4,8},{5,9},{6,10},{7,11},{8,4},{9,5},{10,... | collective-permute-start | bytes 344072 | tf_op jit(solution)/shard_map/ppermute | solution.py:332
  9.1 8.9 %collective-permute-start.4 = (f32[6,16,128]{2,1,0:T(8,128)S(1)}, f32[6,16,128]{2,1,0:T(8,128)S(1)}, u32[]{:S(2)}, u32[]{:S(2)}) collective-permute-start(f32[6,16,128]{2,1,0:T(8,128)S(1)} %get-tuple-element.23), channel_id=1, source_target_pairs={{0,8},{1,9},{2,3},{3,2},{4,12},{5,13},{6,7},{7,6},{8,0},{9,1},{10,... | collective-permute-start | bytes 147464 | tf_op jit(solution)/shard_map/ppermute | solution.py:325
  11.7 6.3 %collective-permute-start.5 = (f32[6,16,128]{2,1,0:T(8,128)S(1)}, f32[6,16,128]{2,1,0:T(8,128)S(1)}, u32[]{:S(2)}, u32[]{:S(2)}) collective-permute-start(f32[6,16,128]{2,1,0:T(8,128)S(1)} %get-tuple-element.24), channel_id=1, source_target_pairs={{0,10},{1,11},{2,0},{3,1},{4,14},{5,15},{6,4},{7,5},{8,2},{9,3},{1... | collective-permute-start | bytes 147464 | tf_op jit(solution)/shard_map/ppermute | solution.py:325
  12.6 1.2 %collective-permute-start = (f32[1,8,128]{2,1,0:T(8,128)S(1)}, f32[1,8,128]{2,1,0:T(8,128)S(1)}, u32[]{:S(2)}, u32[]{:S(2)}) collective-permute-start(f32[1,8,128]{2,1,0:T(8,128)S(1)} %get-tuple-element.17.refs_0_), channel_id=1, source_target_pairs={{0,1},{1,0},{2,3},{3,2},{4,5},{5,4},{6,7},{7,6},{8,9},{9,8},{10,11... | collective-permute-start | bytes 12296 | tf_op jit(solution)/shard_map/ppermute | solution.py:300
  20.2 4.0 %collective-permute-start.6 = (f32[4,16,128]{2,1,0:T(8,128)S(1)}, f32[4,16,128]{2,1,0:T(8,128)S(1)}, u32[]{:S(2)}, u32[]{:S(2)}) collective-permute-start(f32[4,16,128]{2,1,0:T(8,128)S(1)} %get-tuple-element.26), channel_id=1, source_target_pairs={{0,2},{1,3},{2,0},{3,1},{4,6},{5,7},{6,4},{7,5},{8,10},{9,11},{10,... | collective-permute-start | bytes 98312 | tf_op jit(solution)/shard_map/ppermute | solution.py:300
  22.2 1.9 %collective-permute-start.7 = (f32[4,16,128]{2,1,0:T(8,128)S(1)}, f32[4,16,128]{2,1,0:T(8,128)S(1)}, u32[]{:S(2)}, u32[]{:S(2)}) collective-permute-start(f32[4,16,128]{2,1,0:T(8,128)S(1)} %get-tuple-element.27), channel_id=1, source_target_pairs={{0,1},{1,0},{2,3},{3,2},{4,5},{5,4},{6,7},{7,6},{8,9},{9,8},{10,11... | collective-permute-start | bytes 98312 | tf_op jit(solution)/shard_map/ppermute | solution.py:300
  22.2 3.3 %collective-permute-start.8 = (f32[4,16,128]{2,1,0:T(8,128)S(1)}, f32[4,16,128]{2,1,0:T(8,128)S(1)}, u32[]{:S(2)}, u32[]{:S(2)}) collective-permute-start(f32[4,16,128]{2,1,0:T(8,128)S(1)} %get-tuple-element.28), channel_id=1, source_target_pairs={{0,3},{1,2},{2,1},{3,0},{4,7},{5,6},{6,5},{7,4},{8,11},{9,10},{10,... | collective-permute-start | bytes 98312 | tf_op jit(solution)/shard_map/ppermute | solution.py:300
